TPU v7x, 32 devices: a whole 2x2x4 slice. The times are simulated.
32 devices in a mesh: ctx: 8 (over z, x), head: 4 (over y, core).
Axes of the slice: x: 2, y: 2, z: 4, core: 2. Of those that a mesh axis runs over, the one named last changes fastest.
Arguments:
- q_latent: bfloat16 [1024, 1536], P('ctx'), may hold values from -6 to 6
- latent_bias: float32 [8, 1536], P('ctx'), may hold values from -3 to 3
- norm_gain: float32 [1536], replicated, may hold values from 0.5 to 1.5
- w_q: bfloat16 [1536, 24576], P('ctx', 'head'), may hold values from -0.15625 to 0.15625
- steer: float32 [8, 24576], P('ctx', 'head'), may hold values from -10 to 10
- kv_latent: bfloat16 [1024, 512], P('ctx'), may hold values from -6 to 6
- key_rope: bfloat16 [1024, 64], P('ctx'), may hold values from -10 to 10
- w_uk: bfloat16 [512, 16384], P(None, 'head'), may hold values from -0.25 to 0.25
- w_uv: bfloat16 [512, 16384], P(None, 'head'), may hold values from -0.25 to 0.25
- d_out: bfloat16 [1024, 16384], P('ctx', 'head'), may hold values from -0.29882812 to 0.29882812
- block_mask: int32 [8, 8], replicated, may hold values from 0 to 1, as said below
Outputs:
- grad_steer: float32 [8, 24576], P('ctx', 'head')
- grad_latent_bias: float32 [8, 1536], P('ctx')
Inputs may be any that keep to these rules, and one draw needn't show every extreme that they name: `block_mask`: query block i always attends key block i; its other entries are 1 at a rate drawn per query block among 1/16, 2/16, 4/16 and 7/16.
All inputs are finite; a program needn't handle non-finite values.
Results may differ from a plain program's by a relative error of at most 0.024.
Values may be sent and summed in bfloat16 or wider, within the bound.
No kernel may reach another device: no remote copies, remote signals or barrier semaphores. Data moves between devices by JAX's collectives and lax.ppermute only.
A program may use at most 128 MiB of HBM per device.

v0:
```python
import math

import jax
import jax.numpy as jnp
from jax import lax
from jax.experimental import pallas as pl
from jax.experimental.pallas import tpu as pltpu
from jax.sharding import PartitionSpec as P

KVL = 512
NOPE = 128
ROPE = 64
VD = 128
BLK = 128


epsilon = 1e-06
lowest = -1e30


def contract_last(left, right):
    return lax.dot_general(
        left, right, (((1,), (1,)), ((), ())), preferred_element_type=jnp.float32
    )


def shards(
    q_latent, latent_bias, norm_gain, w_q, steer, kv_latent, key_rope, w_uk, w_uv, d_out, block_mask
):
    queries = q_latent.shape[0]
    nblocks = queries // BLK
    head_count = w_uk.shape[1] // NOPE
    head_width = NOPE + ROPE
    score_scale = head_width ** (-0.5)
    row_count = queries * head_count
    shifted = q_latent.astype(jnp.float32) + jnp.repeat(latent_bias, BLK, axis=0)
    inv_rms = lax.rsqrt(jnp.mean(shifted * shifted, axis=1, keepdims=True) + epsilon)
    normed = shifted * inv_rms
    c_query = (normed * norm_gain).astype(jnp.bfloat16)
    full_wq = lax.all_gather(w_q, "ctx", axis=0, tiled=True)
    projected = jnp.dot(c_query, full_wq, preferred_element_type=jnp.float32)
    query_all = (
        (projected + jnp.repeat(steer, BLK, axis=0))
        .astype(jnp.bfloat16)
        .reshape(queries, head_count, head_width)
    )
    q_rope = query_all[:, :, NOPE:].reshape(row_count, ROPE)
    key_up = w_uk.reshape(KVL, head_count, NOPE)
    value_up = w_uv.reshape(KVL, head_count, VD)
    q_absorbed = (
        jnp.einsum(
            "qhn,khn->qhk", query_all[:, :, :NOPE], key_up, preferred_element_type=jnp.float32
        )
        .astype(jnp.bfloat16)
        .reshape(row_count, KVL)
    )
    g_absorbed = (
        jnp.einsum(
            "qhv,khv->qhk",
            d_out.reshape(queries, head_count, VD),
            value_up,
            preferred_element_type=jnp.float32,
        )
        .astype(jnp.bfloat16)
        .reshape(row_count, KVL)
    )
    my_mask = lax.dynamic_slice_in_dim(block_mask, lax.axis_index("ctx") * nblocks, nblocks, 0)
    start_status = (
        jnp.full((row_count,), lowest, jnp.float32),
        jnp.zeros((row_count,), jnp.float32),
        jnp.zeros((row_count,), jnp.float32),
        jnp.zeros((2 * row_count, KVL), jnp.float32),
        jnp.zeros((2 * row_count, ROPE), jnp.float32),
    )
    lat_portion = lax.all_gather(kv_latent, "ctx", axis=0, tiled=True)
    rope_portion = lax.all_gather(key_rope, "ctx", axis=0, tiled=True)
    key_total = lat_portion.shape[0]
    tile_len = math.gcd(key_total, BLK)
    tile_count = key_total // tile_len

    def visit_tile(status, inputs):
        lat_tile, rope_tile, offset = inputs
        key_block = offset * tile_len // BLK
        column = lax.dynamic_index_in_dim(my_mask, key_block, 1, keepdims=False)

        def update(status):
            peak, total_weight, weighted, lat_acc, rope_acc = status
            live_rows = jnp.repeat(column > 0, head_count * BLK)[:, None]
            scores = (
                contract_last(q_absorbed, lat_tile) + contract_last(q_rope, rope_tile)
            ) * score_scale
            scores = jnp.where(live_rows, scores, lowest)
            new_peak = jnp.maximum(peak, jnp.max(scores, axis=1))
            factor = jnp.exp(peak - new_peak)
            weights = jnp.where(live_rows, jnp.exp(scores - new_peak[:, None]), 0.0)
            dots = contract_last(g_absorbed, lat_tile)
            mixed = weights * dots
            total_weight = total_weight * factor + jnp.sum(weights, axis=1)
            weighted = weighted * factor + jnp.sum(mixed, axis=1)
            stacked = jnp.concatenate([mixed, weights], axis=0).astype(jnp.bfloat16)
            doubled = jnp.concatenate([factor, factor])[:, None]
            lat_acc = lat_acc * doubled + jnp.dot(
                stacked, lat_tile, preferred_element_type=jnp.float32
            )
            rope_acc = rope_acc * doubled + jnp.dot(
                stacked, rope_tile, preferred_element_type=jnp.float32
            )
            return (new_peak, total_weight, weighted, lat_acc, rope_acc)

        def keep_status(status):
            return status

        return (lax.cond(jnp.max(column) > 0, update, keep_status, status), None)

    offsets = jnp.arange(tile_count, dtype=jnp.int32)
    tiles = (
        lat_portion.reshape(tile_count, tile_len, KVL),
        rope_portion.reshape(tile_count, tile_len, ROPE),
        offsets,
    )
    result, _ = lax.scan(visit_tile, start_status, tiles)
    _, total_weight, weighted, lat_acc, rope_acc = result
    ratio = (weighted / total_weight)[:, None]
    inverse = (score_scale / total_weight)[:, None]
    grad_lat = ((lat_acc[:row_count] - ratio * lat_acc[row_count:]) * inverse).astype(jnp.bfloat16)
    grad_rope = (rope_acc[:row_count] - ratio * rope_acc[row_count:]) * inverse
    grad_nope = jnp.einsum(
        "qhk,khn->qhn",
        grad_lat.reshape(queries, head_count, KVL),
        key_up,
        preferred_element_type=jnp.float32,
    )
    grad_query = jnp.concatenate(
        [grad_nope, grad_rope.reshape(queries, head_count, ROPE)], axis=2
    ).reshape(queries, head_count * head_width)
    grad_steer = jnp.sum(grad_query.reshape(nblocks, BLK, head_count * head_width), axis=1)
    grad_round = grad_query.astype(jnp.bfloat16)
    partial_grad = contract_last(grad_round, full_wq)
    latent_grad = lax.psum(partial_grad.astype(jnp.bfloat16), "head").astype(jnp.float32)
    scaled = latent_grad * norm_gain
    project_mean = jnp.mean(scaled * normed, axis=1, keepdims=True)
    grad_shifted = inv_rms * (scaled - normed * project_mean)
    grad_bias = jnp.sum(grad_shifted.reshape(nblocks, BLK, grad_shifted.shape[1]), axis=1)
    return (grad_steer, grad_bias)


WIDE = 256
PIECE = 32
UNROLL = 2
VMEM_LIMIT = 60 * 1024 * 1024
f32 = jnp.float32
bf16 = jnp.bfloat16


def dot(left, right):
    return jnp.dot(left, right, preferred_element_type=f32)


def prep_kernel(pick, lat_ref, bias_ref, gain_ref, kv_ref, rope_ref, out_ref):
    ql = lat_ref.shape[1]
    shifted = lat_ref[...].astype(f32) + bias_ref[...]
    inv = lax.rsqrt(jnp.mean(shifted * shifted, axis=1, keepdims=True) + epsilon)
    out_ref[:, :ql] = (shifted * inv * gain_ref[...]).astype(bf16)
    out_ref[:, ql : ql + KVL] = kv_ref[...]
    out_ref[:, ql + KVL : ql + KVL + ROPE] = rope_ref[...]
    high = inv.astype(bf16)
    low = (inv - high.astype(f32)).astype(bf16)
    lane = lax.broadcasted_iota(jnp.int32, (lat_ref.shape[0], ROPE), 1)
    pair = jnp.where(lane == 0, high.astype(f32), jnp.where(lane == 1, low.astype(f32), 0.0))
    out_ref[:, ql + KVL + ROPE :] = pair.astype(bf16)


def keys_kernel(place, near_ref, far_ref, uk_ref, uv_ref, c_ref, tail_ref, wide_ref, value_ref, kv_ref):
    ql = c_ref.shape[1]
    for position, ref in ((0, near_ref), (1, far_ref)):
        for piece in range(16):
            rows = pl.ds(pl.multiple_of(place[position * 16 + piece], PIECE), PIECE)
            c_ref[rows, :] = ref[piece, :, :ql]
            kv_ref[rows, :] = ref[piece, :, ql : ql + KVL]
            tail_ref[rows, :] = ref[piece, :, ql + KVL :]
    heads = wide_ref.shape[0]
    step = 256
    lane = lax.broadcasted_iota(jnp.int32, (step, NOPE), 1)
    for start in range(0, c_ref.shape[0], step):
        rows = slice(start, start + step)
        kv = kv_ref[rows, :]
        up = dot(kv, uk_ref[...])
        value_ref[rows, :] = dot(kv, uv_ref[...]).astype(bf16)
        rope = jnp.where(lane < ROPE, tail_ref[rows, :].astype(f32), 0.0)
        for head in range(heads):
            full = jnp.concatenate([up[:, head * NOPE : (head + 1) * NOPE], rope], axis=1)
            if head % 2:
                full = pltpu.roll(full, ROPE, 1)
            wide_ref[head, rows, :] = full.astype(bf16)


def query_kernel(place, *refs):
    count = len(refs) - 5
    weights, (c_ref, steer_ref, q_ref, proj_ref, full_ref) = refs[:count], refs[count:]
    depth = weights[0].shape[0]
    for index, ref in enumerate(weights):
        full_ref[pl.ds(pl.multiple_of(place[index] * depth, 64), depth), :] = ref[...]
    step = 256
    for start in range(0, c_ref.shape[0], step):
        projected = dot(c_ref[start : start + step, :], full_ref[...])
        proj_ref[start : start + step, :] = projected
        for part in range(step // BLK):
            block = start // BLK + part
            low = part * BLK
            q_ref[start + low : start + low + BLK, :] = (
                projected[low : low + BLK] + steer_ref[block : block + 1, :]
            ).astype(bf16)


def attend_kernel(mask, place, *refs):
    count = len(refs) - 17
    cots = refs[:count]
    (
        q_ref, proj_ref, tail_ref, wide_ref, value_ref, weight_ref, out_ref,
        cot_ref, sums_ref, weighted_ref, row_ref, score_ref, dot_ref, first_ref, second_ref, grad_ref, pair_ref,
    ) = refs[count:]
    nblocks = count
    heads = wide_ref.shape[0]
    width = NOPE + ROPE
    scale = width ** (-0.5)
    for index, ref in enumerate(cots):
        cot_ref[place[index]] = ref[...]

    def list_step(index, found):
        block, key = index // mask.shape[1], index % mask.shape[1]
        pair_ref[0, found] = block
        pair_ref[1, found] = key
        return found + (mask[block, key] > 0).astype(jnp.int32)

    found = lax.fori_loop(0, nblocks * mask.shape[1], list_step, 0)
    pair_ref[0, found] = nblocks
    pair_ref[1, found] = 0
    trips = (found + UNROLL - 1) // UNROLL

    def each_pair(visit):
        def trip(index, carry):
            for part in range(UNROLL):
                pair = index * UNROLL + part
                visit(pair, pair_ref[0, pair], pair_ref[1, pair])
            return carry

        lax.fori_loop(0, trips, trip, 0)

    def each_block(visit):
        def trip(block, carry):
            visit(block)
            return carry

        lax.fori_loop(0, nblocks, trip, 0)

    def span(block):
        return pl.ds(pl.multiple_of(block * BLK, BLK), BLK)

    first_ref[...] = jnp.full_like(first_ref, lowest)

    def score(pair, block, key):
        rows = span(jnp.minimum(block, nblocks - 1))
        for head in range(heads):
            left = head // 2 * 2 * width + head % 2 * NOPE
            scores = contract_last(q_ref[rows, left : left + WIDE], wide_ref[head, span(key), :]) * scale
            score_ref[pair, head] = scores
            first_ref[block, head] = jnp.maximum(first_ref[block, head], scores)

    each_pair(score)

    peak_ref = grad_ref

    def find_peak(block):
        for head in range(heads):
            peak = jnp.max(first_ref[block, head], axis=1, keepdims=True)
            peak_ref[block, :, head * BLK : (head + 1) * BLK] = jnp.broadcast_to(peak, (BLK, BLK))

    each_block(find_peak)
    peak_ref[nblocks] = jnp.zeros_like(peak_ref[nblocks])
    first_ref[...] = jnp.zeros_like(first_ref)
    second_ref[...] = jnp.zeros_like(second_ref)

    def weigh(pair, block, key):
        source = jnp.minimum(block, nblocks - 1)
        for head in range(heads):
            lanes = slice(head * VD, (head + 1) * VD)
            dots = contract_last(cot_ref[source, :, lanes], value_ref[span(key), lanes])
            weights = jnp.exp(score_ref[pair, head] - peak_ref[block, :, head * BLK : (head + 1) * BLK])
            score_ref[pair, head] = weights
            dot_ref[pair, head] = dots
            first_ref[block, head] = first_ref[block, head] + weights
            second_ref[block, head] = second_ref[block, head] + weights * dots

    each_pair(weigh)

    def normalise(block):
        for head in range(heads):
            total = jnp.sum(first_ref[block, head], axis=1, keepdims=True)
            mixed = jnp.sum(second_ref[block, head], axis=1, keepdims=True)
            first_ref[block, head] = jnp.broadcast_to(scale / total, (BLK, BLK))
            second_ref[block, head] = jnp.broadcast_to(mixed / total, (BLK, BLK))

    each_block(normalise)
    grad_ref[...] = jnp.zeros_like(grad_ref)

    def gather(pair, block, key):
        for head in range(heads):
            left = head // 2 * 2 * width + head % 2 * NOPE
            slope = score_ref[pair, head] * (dot_ref[pair, head] - second_ref[block, head])
            slope = (slope * first_ref[block, head]).astype(bf16)
            lanes = slice(left, left + WIDE)
            grad_ref[block, :, lanes] = grad_ref[block, :, lanes] + dot(slope, wide_ref[head, span(key), :])

    each_pair(gather)

    def reduce(block):
        grad = grad_ref[block]
        tail = tail_ref[span(block), :].astype(f32)
        inv = tail[:, ROPE : ROPE + 1] + tail[:, ROPE + 1 : ROPE + 2]
        sums_ref[pl.ds(block, 1), :] = jnp.sum(grad, axis=0, keepdims=True)
        weighted_ref[pl.ds(block, 1), :] = jnp.sum(grad * inv, axis=0, keepdims=True)
        products = grad * proj_ref[span(block), :]
        narrow = products[:, :128]
        for start in range(128, products.shape[1], 128):
            narrow = narrow + products[:, start : start + 128]
        row_ref[pl.ds(block, 1), :] = jnp.sum(narrow.T, axis=0, keepdims=True)

    each_block(reduce)
    weighted = weighted_ref[...]
    high = weighted.astype(bf16)
    low = (weighted - high.astype(f32)).astype(bf16)
    both = contract_last(jnp.concatenate([high, low], axis=0), weight_ref[...])
    back = both[:nblocks] + both[nblocks:]
    out_ref[...] = jnp.zeros_like(out_ref)
    chunks = []
    for array in (back, row_ref[...], sums_ref[...]):
        for start in range(0, array.shape[1], 128):
            chunks.append(array[:, start : start + 128])
    for index, chunk in enumerate(chunks):
        for block in range(nblocks):
            out_ref[block, index : index + 1, :] = chunk[block : block + 1, :]


def full(shape):
    return pl.BlockSpec(shape, lambda *unused: (0,) * len(shape))


def params():
    return pltpu.CompilerParams(vmem_limit_bytes=VMEM_LIMIT)


def cost(flops, moved):
    return pl.CostEstimate(flops=flops, bytes_accessed=moved, transcendentals=0)


def spread(
    ring, head_shards, q_latent, latent_bias, norm_gain, w_q, steer, kv_latent, key_rope, w_uk, w_uv, d_out, block_mask
):
    ql = q_latent.shape[1]
    queries = ring * BLK
    mine = lax.axis_index("ctx")
    lane = lax.axis_index("head")
    columns = w_q.shape[1] // ring
    cot_columns = d_out.shape[1] // ring
    heads = cot_columns // VD
    shifts = range(1, ring)

    def chunk(array, width, step):
        return lax.dynamic_slice_in_dim(array, (mine + step) % ring * width, width, 1)

    def send(array, axis, target, size):
        return lax.ppermute(array, axis, [(i, target(i)) for i in range(size)])

    def turn(array, step):
        return send(array, "ctx", lambda i: (i + step) % ring, ring)

    gain_row = norm_gain[None, :]
    payload_width = ql + KVL + 2 * ROPE
    piece = pl.pallas_call(
        prep_kernel,
        out_shape=jax.ShapeDtypeStruct((PIECE, payload_width), bf16),
        grid_spec=pltpu.PrefetchScalarGridSpec(
            num_scalar_prefetch=1,
            grid=(1,),
            in_specs=[
                pl.BlockSpec((PIECE, ql), lambda i, pick: (pick[0], 0)),
                full((1, ql)),
                full((1, ql)),
                pl.BlockSpec((PIECE, KVL), lambda i, pick: (pick[0], 0)),
                pl.BlockSpec((PIECE, ROPE), lambda i, pick: (pick[0], 0)),
            ],
            out_specs=full((PIECE, payload_width)),
        ),
        cost_estimate=cost(10**6, 10**6),
    )(lane[None], q_latent, latent_bias, gain_row, kv_latent, key_rope)
    pieces = [piece] + [turn(piece, 2 * step) for step in range(1, ring // 2)]
    weight_parts = [chunk(w_q, columns, 0)] + [turn(chunk(w_q, columns, step), step) for step in shifts]
    first = jnp.stack(pieces)
    second = send(first, "ctx", lambda i: i ^ 1, ring)
    both = jnp.concatenate([first, second])
    other = send(both, "head", lambda i: i ^ 2, head_shards)
    near = jnp.concatenate([both, other])
    far = send(near, "head", lambda i: i ^ 1, head_shards)
    cot_parts = [chunk(d_out, cot_columns, 0)] + [turn(chunk(d_out, cot_columns, step), step) for step in shifts]
    all_steer = lax.all_to_all(steer.reshape(ring, columns), "ctx", 0, 0, tiled=True)

    z, x = mine // 2, mine % 2
    places = []
    for core in range(2):
        for y in range(2):
            for dx in range(2):
                for step in range(ring // 2):
                    block = (z + ring // 2 - step) % (ring // 2) * 2 + (x + dx) % 2
                    places.append(block * BLK + PIECE * (lane ^ (2 * y + core)))
    places = jnp.stack(places).astype(jnp.int32)
    sources = jnp.stack([(mine + ring - step) % ring for step in range(ring)]).astype(jnp.int32)

    c_query, tail, wide, values = pl.pallas_call(
        keys_kernel,
        out_shape=(
            jax.ShapeDtypeStruct((queries, ql), bf16),
            jax.ShapeDtypeStruct((queries, 2 * ROPE), bf16),
            jax.ShapeDtypeStruct((heads, queries, WIDE), bf16),
            jax.ShapeDtypeStruct((queries, heads * VD), bf16),
        ),
        grid_spec=pltpu.PrefetchScalarGridSpec(
            num_scalar_prefetch=1,
            grid=(1,),
            in_specs=[
                full((16, PIECE, payload_width)),
                full((16, PIECE, payload_width)),
                pl.BlockSpec((KVL, heads * NOPE), lambda i, place: (0, place[32])),
                pl.BlockSpec((KVL, heads * VD), lambda i, place: (0, place[32])),
            ],
            out_specs=(
                full((queries, ql)),
                full((queries, 2 * ROPE)),
                full((heads, queries, WIDE)),
                full((queries, heads * VD)),
            ),
            scratch_shapes=[pltpu.VMEM((queries, KVL), bf16)],
        ),
        compiler_params=params(),
        cost_estimate=cost(2 * 10**9, 10**7),
    )(jnp.concatenate([places, mine[None]]), near, far, w_uk, w_uv)

    query, projected, weight = pl.pallas_call(
        query_kernel,
        out_shape=(
            jax.ShapeDtypeStruct((queries, columns), bf16),
            jax.ShapeDtypeStruct((queries, columns), f32),
            jax.ShapeDtypeStruct((ql, columns), bf16),
        ),
        grid_spec=pltpu.PrefetchScalarGridSpec(
            num_scalar_prefetch=1,
            grid=(1,),
            in_specs=[full(weight_parts[0].shape)] * ring + [full((queries, ql)), full((ring, columns))],
            out_specs=(full((queries, columns)), full((queries, columns)), full((ql, columns))),
        ),
        compiler_params=params(),
        cost_estimate=cost(3 * 10**9, 10**7),
    )(sources, *weight_parts, c_query, all_steer)

    used = (ql + BLK + columns) // 128
    slots = (used + 7) // 8 * 8
    pairs = (ring * ring + UNROLL - 1) // UNROLL * UNROLL
    sums = pl.pallas_call(
        attend_kernel,
        out_shape=jax.ShapeDtypeStruct((ring, slots, 128), f32),
        grid_spec=pltpu.PrefetchScalarGridSpec(
            num_scalar_prefetch=2,
            grid=(1,),
            in_specs=[full((BLK, cot_columns))] * ring
            + [
                full((queries, columns)),
                full((queries, columns)),
                full((queries, 2 * ROPE)),
                full((heads, queries, WIDE)),
                full((queries, heads * VD)),
                full((ql, columns)),
            ],
            out_specs=full((ring, slots, 128)),
            scratch_shapes=[
                pltpu.VMEM((ring, BLK, cot_columns), bf16),
                pltpu.VMEM((ring, columns), f32),
                pltpu.VMEM((ring, columns), f32),
                pltpu.VMEM((ring, BLK), f32),
                pltpu.VMEM((pairs, heads, BLK, BLK), f32),
                pltpu.VMEM((pairs, heads, BLK, BLK), f32),
                pltpu.VMEM((ring + 1, heads, BLK, BLK), f32),
                pltpu.VMEM((ring + 1, heads, BLK, BLK), f32),
                pltpu.VMEM((ring + 1, BLK, columns), f32),
                pltpu.SMEM((2, pairs + UNROLL), jnp.int32),
            ],
        ),
        compiler_params=params(),
        cost_estimate=cost(8 * 10**9, 10**7),
    )(block_mask, sources, *cot_parts, query, projected, tail, wide, values, weight)

    arrived = lax.all_to_all(sums, "ctx", 0, 0, tiled=True)
    cut = (ql + BLK) // 128
    grad_steer = arrived[:, cut:used].reshape(1, ring * columns)
    local = jnp.sum(arrived[:, :cut], axis=0)
    summed = local
    for bits in range(1, head_shards):
        summed = summed + lax.ppermute(local, "head", [(i, i ^ bits) for i in range(head_shards)])
    back = summed[: ql // 128].reshape(1, ql)
    dots = summed[ql // 128 : cut].reshape(BLK, 1)
    shifted = q_latent.astype(f32) + latent_bias
    inv = lax.rsqrt(jnp.mean(shifted * shifted, axis=1, keepdims=True) + epsilon)
    pull = jnp.sum(shifted * (inv * inv * dots / ql), axis=0, keepdims=True)
    return (grad_steer, back * gain_row - pull)


def solution(mesh):
    ring, head_shards = mesh.shape["ctx"], mesh.shape["head"]

    def body(*arrays):
        heads = arrays[7].shape[1] // NOPE
        fits = arrays[0].shape[0] == BLK and ring == 8 and head_shards == 4 and heads % (2 * ring) == 0
        if fits:
            return spread(ring, head_shards, *arrays)
        return shards(*arrays)

    in_specs = (
        P("ctx", None),
        P("ctx", None),
        P(),
        P("ctx", "head"),
        P("ctx", "head"),
        P("ctx", None),
        P("ctx", None),
        P(None, "head"),
        P(None, "head"),
        P("ctx", "head"),
        P(),
    )
    out_specs = (P("ctx", "head"), P("ctx", None))
    return jax.shard_map(body, mesh=mesh, in_specs=in_specs, out_specs=out_specs, check_vma=False)
```

profile of v0, /device:TPU:0, one launch (start us, length us, event | category | flops | bytes accessed | tf_op | source)
XLA Modules:
  0.0 200.1 jit_solution(13254731205243050730)
XLA Ops:
  0.6 1.4 copy.15.rope_ref
  2.1 1.3 broadcast_in_dim.13.gain_ref
  3.4 1.8 shard_map.122
  5.1 3.1 %collective-permute-start.14 = (bf16[32,2176]{1,0:T(8,128)(2,1)}, bf16[32,2176]{1,0:T(8,128)(2,1)S(1)}, u32[]{:S(2)}, u32[]{:S(2)}) collective-permute-start(bf16[32,2176]{1,0:T(8,128)(2,1)} %shard_map.122), channel_id=1, source_target_pairs={{0,8},{4,12},{8,16},{12,20},{16,24},{20,28},{24,0},{28,4},{1,9},{5... | collective-permute-start | bytes 417800 | tf_op jit(solution)/shard_map/ppermute | solution.py:372
  8.2 2.6 %collective-permute-start.15 = (bf16[32,2176]{1,0:T(8,128)(2,1)}, bf16[32,2176]{1,0:T(8,128)(2,1)S(1)}, u32[]{:S(2)}, u32[]{:S(2)}) collective-permute-start(bf16[32,2176]{1,0:T(8,128)(2,1)} %shard_map.122), channel_id=1, source_target_pairs={{0,16},{4,20},{8,24},{12,28},{16,0},{20,4},{24,8},{28,12},{1,17},{... | collective-permute-start | bytes 417800 | tf_op jit(solution)/shard_map/ppermute | solution.py:372
  10.8 1.3 collective-permute-start.16
  13.1 2.0 collective-permute-done.14
  15.0 5.1 %collective-permute-done.15 = bf16[32,2176]{1,0:T(8,128)(2,1)S(1)} collective-permute-done((bf16[32,2176]{1,0:T(8,128)(2,1)}, bf16[32,2176]{1,0:T(8,128)(2,1)S(1)}, u32[]{:S(2)}, u32[]{:S(2)}) %collective-permute-start.15) | collective-permute-done | bytes 139296 | tf_op jit(solution)/shard_map/ppermute | solution.py:372
  21.2 1.6 collective-permute-start.17
  22.8 12.9 %collective-permute-done.17 = bf16[4,32,2176]{2,1,0:T(8,128)(2,1)S(1)} collective-permute-done((bf16[4,32,2176]{2,1,0:T(8,128)(2,1)S(1)}, bf16[4,32,2176]{2,1,0:T(8,128)(2,1)S(1)}, u32[]{:S(2)}, u32[]{:S(2)}) %collective-permute-start.17) | collective-permute-done | bytes 557088 | tf_op jit(solution)/shard_map/ppermute | solution.py:372
  35.8 1.6 collective-permute-start.18
  37.4 24.0 %collective-permute-done.18 = bf16[8,32,2176]{2,1,0:T(8,128)(2,1)S(1)} collective-permute-done((bf16[8,32,2176]{2,1,0:T(8,128)(2,1)S(1)}, bf16[8,32,2176]{2,1,0:T(8,128)(2,1)S(1)}, u32[]{:S(2)}, u32[]{:S(2)}) %collective-permute-start.18) | collective-permute-done | bytes 1114144 | tf_op jit(solution)/shard_map/ppermute | solution.py:372
  61.8 3.7 %constant_dynamic-slice_fusion = (bf16[192,768]{1,0:T(8,128)(2,1)}, bf16[192,768]{1,0:T(8,128)(2,1)}, bf16[192,768]{1,0:T(8,128)(2,1)}, bf16[192,768]{1,0:T(8,12...) fusion(bf16[192,6144]{1,0:T(8,128)(2,1)} %param.14, ...), kind=kLoop, calls=%fused_computation.21 | loop fusion | bytes 4718624 | tf_op jit(solution)/shard_map/dynamic_slice | solution.py:369
  65.5 2.8 %collective-permute-start.10 = (bf16[192,768]{1,0:T(8,128)(2,1)}, bf16[192,768]{1,0:T(8,128)(2,1)}, u32[]{:S(2)}, u32[]{:S(2)}) collective-permute-start(bf16[192,768]{1,0:T(8,128)(2,1)} %get-tuple-element.18), channel_id=1, source_target_pairs={{0,16},{4,20},{8,24},{12,28},{16,0},{20,4},{24,8},{28,12},{1,17},{... | collective-permute-start | bytes 884744 | tf_op jit(solution)/shard_map/ppermute | solution.py:372
  68.2 1.1 collective-permute-start.11
  70.2 3.6 %collective-permute-start = (bf16[128,512]{1,0:T(8,128)(2,1)S(1)}, bf16[128,512]{1,0:T(8,128)(2,1)S(1)}, u32[]{:S(2)}, u32[]{:S(2)}) collective-permute-start(bf16[128,512]{1,0:T(8,128)(2,1)S(1)} %get-tuple-element.29), channel_id=1, source_target_pairs={{0,4},{4,8},{8,12},{12,16},{16,20},{20,24},{24,28},{28,0},{1,5},{5... | collective-permute-start | bytes 393224 | tf_op jit(solution)/shard_map/ppermute | solution.py:372
  73.9 15.8 %collective-permute-done.refs_1_ = bf16[128,512]{1,0:T(8,128)(2,1)S(1)} collective-permute-done((bf16[128,512]{1,0:T(8,128)(2,1)S(1)}, bf16[128,512]{1,0:T(8,128)(2,1)S(1)}, u32[]{:S(2)}, u32[]{:S(2)}) %collective-permute-start) | collective-permute-done | bytes 131104 | tf_op jit(solution)/shard_map/ppermute | solution.py:372
  89.7 9.5 %collective-permute-start.12 = (bf16[192,768]{1,0:T(8,128)(2,1)}, bf16[192,768]{1,0:T(8,128)(2,1)S(1)}, u32[]{:S(2)}, u32[]{:S(2)}) collective-permute-start(bf16[192,768]{1,0:T(8,128)(2,1)} %get-tuple-element.23), channel_id=1, source_target_pairs={{0,24},{4,28},{8,0},{12,4},{16,8},{20,12},{24,16},{28,20},{1,25},{... | collective-permute-start | bytes 884744 | tf_op jit(solution)/shard_map/ppermute | solution.py:372
  99.9 1.4 collective-permute-start.13
  101.9 1.6 collective-permute-start.8
  103.5 4.0 %collective-permute-start.9 = (bf16[192,768]{1,0:T(8,128)(2,1)}, bf16[192,768]{1,0:T(8,128)(2,1)S(1)}, u32[]{:S(2)}, u32[]{:S(2)}) collective-permute-start(bf16[192,768]{1,0:T(8,128)(2,1)} %get-tuple-element.19), channel_id=1, source_target_pairs={{0,12},{4,16},{8,20},{12,24},{16,28},{20,0},{24,4},{28,8},{1,13},{... | collective-permute-start | bytes 884744 | tf_op jit(solution)/shard_map/ppermute | solution.py:372
  107.5 3.3 %all-to-all-start = ((f32[8,1,768]{2,1,0:T(1,128)}), f32[8,1,768]{2,1,0:T(1,128)S(1)}, u32[]{:S(2)}, u32[]{:S(2)}) async-start(f32[8,1,768]{2,1,0:T(1,128)} %bitcast.74), calls=%async_computation | async-start | bytes 49152 | tf_op jit(solution)/shard_map/all_to_all | solution.py:405
  112.2 20.4 %all-to-all-done = f32[8,1,768]{2,1,0:T(1,128)S(1)} async-done(((f32[8,1,768]{2,1,0:T(1,128)}), f32[8,1,768]{2,1,0:T(1,128)S(1)}, u32[]{:S(2)}, u32[]{:S(2)}) %all-to-all-start) | async-done | bytes 24608 | tf_op jit(solution)/shard_map/all_to_all | solution.py:405
  133.3 7.4 %shard_map.123 = (bf16[1024,1536]{1,0:T(8,128)(2,1)}, bf16[1024,128]{1,0:T(8,128)(2,1)}, bf16[4,1024,256]{2,1,0:T(8,128)(2,1)}, bf16[1024,512]{1,0:T(8,128)(2,1)}) custom-call(s32[33]{0:T(128)} %concatenate.11.place, bf16[16,32,2176]{2,1,0:T(8,128)(2,1)} %copy-done.1, bf16[16,32,2176]{2,1,0:T(8,128)(2,1)} %collective-permute-done.19.far_ref, ...), custom_call_target="tpu_custom_call" | custom-call | flops 2000000000 | bytes 10000000 | tf_op jit(solution)/shard_map/pallas_call | solution.py:418
  142.3 2.4 %collective-permute-start.4 = (bf16[128,512]{1,0:T(8,128)(2,1)S(1)}, bf16[128,512]{1,0:T(8,128)(2,1)S(1)}, u32[]{:S(2)}, u32[]{:S(2)}) collective-permute-start(bf16[128,512]{1,0:T(8,128)(2,1)S(1)} %copy-done.3), channel_id=1, source_target_pairs={{0,20},{4,24},{8,28},{12,0},{16,4},{20,8},{24,12},{28,16},{1,21},{... | collective-permute-start | bytes 393224 | tf_op jit(solution)/shard_map/ppermute | solution.py:372
  144.7 3.0 %collective-permute-start.5 = (bf16[128,512]{1,0:T(8,128)(2,1)S(1)}, bf16[128,512]{1,0:T(8,128)(2,1)S(1)}, u32[]{:S(2)}, u32[]{:S(2)}) collective-permute-start(bf16[128,512]{1,0:T(8,128)(2,1)S(1)} %get-tuple-element.31), channel_id=1, source_target_pairs={{0,24},{4,28},{8,0},{12,4},{16,8},{20,12},{24,16},{28,20},{1,25},{... | collective-permute-start | bytes 393224 | tf_op jit(solution)/shard_map/ppermute | solution.py:372
  147.7 1.5 collective-permute-start.6
  149.2 8.9 %shard_map.124 = (bf16[1024,768]{1,0:T(8,128)(2,1)}, f32[1024,768]{1,0:T(8,128)}, bf16[1536,768]{1,0:T(8,128)(2,1)}) custom-call(s32[8]{0:T(128)} %stack.146.place, bf16[192,768]{1,0:T(8,128)(2,1)} %get-tuple-element.22.refs_0_, bf16[192,768]{1,0:T(8,128)(2,1)} %copy-done.10, bf16[192,768]{1,0:T(8,128)(2,1)} %collective-permute-done.8.refs_2_, ...), custom_call_target="tpu_custom_call" | custom-call | flops 3000000000 | bytes 10000000 | tf_op jit(solution)/shard_map/pallas_call | solution.py:447
  158.9 21.0 %shard_map.125 = f32[8,24,128]{2,1,0:T(8,128)} custom-call(s32[8,8]{1,0:T(8,128)} %mask.1, s32[8]{0:T(128)} %stack.146.place, bf16[128,512]{1,0:T(8,128)(2,1)} %get-tuple-element.30.refs_0_, bf16[128,512]{1,0:T(8,128)(2,1)} %copy-done.12, bf16[128,512]{1,0:T(8,128)(2,1)} %copy-done.13, bf16[128,512]{1,0:T(8,128)(2,1)} %copy-done.14, ...), custom_call_target="tpu_custom_call" | custom-call | flops 8000000000 | bytes 10000000 | tf_op jit(solution)/shard_map/pallas_call | solution.py:467
  179.9 7.5 %all-to-all-start.1 = ((f32[8,24,128]{2,1,0:T(8,128)}), f32[8,24,128]{2,1,0:T(8,128)S(1)}, u32[]{:S(2)}, u32[]{:S(2)}) async-start(f32[8,24,128]{2,1,0:T(8,128)} %shard_map.125), calls=%async_computation.1 | async-start | bytes 196608 | tf_op jit(solution)/shard_map/all_to_all | solution.py:500
  187.5 7.1 %all-to-all-done.1 = f32[8,24,128]{2,1,0:T(8,128)S(1)} async-done(((f32[8,24,128]{2,1,0:T(8,128)}), f32[8,24,128]{2,1,0:T(8,128)S(1)}, u32[]{:S(2)}, u32[]{:S(2)}) %all-to-all-start.1) | async-done | bytes 98336 | tf_op jit(solution)/shard_map/all_to_all | solution.py:500
  194.7 1.6 collective-permute-start.21
  (84 shorter events, 12.8 us)
Async XLA Ops:
  5.1 9.9 %collective-permute-start.14 = (bf16[32,2176]{1,0:T(8,128)(2,1)}, bf16[32,2176]{1,0:T(8,128)(2,1)S(1)}, u32[]{:S(2)}, u32[]{:S(2)}) collective-permute-start(bf16[32,2176]{1,0:T(8,128)(2,1)} %shard_map.122), channel_id=1, source_target_pairs={{0,8},{4,12},{8,16},{12,20},{16,24},{20,28},{24,0},{28,4},{1,9},{5... | collective-permute-start | bytes 417800 | tf_op jit(solution)/shard_map/ppermute | solution.py:372
  8.2 12.0 %collective-permute-start.15 = (bf16[32,2176]{1,0:T(8,128)(2,1)}, bf16[32,2176]{1,0:T(8,128)(2,1)S(1)}, u32[]{:S(2)}, u32[]{:S(2)}) collective-permute-start(bf16[32,2176]{1,0:T(8,128)(2,1)} %shard_map.122), channel_id=1, source_target_pairs={{0,16},{4,20},{8,24},{12,28},{16,0},{20,4},{24,8},{28,12},{1,17},{... | collective-permute-start | bytes 417800 | tf_op jit(solution)/shard_map/ppermute | solution.py:372
  10.8 9.4 %collective-permute-start.16 = (bf16[32,2176]{1,0:T(8,128)(2,1)}, bf16[32,2176]{1,0:T(8,128)(2,1)S(1)}, u32[]{:S(2)}, u32[]{:S(2)}) collective-permute-start(bf16[32,2176]{1,0:T(8,128)(2,1)} %shard_map.122), channel_id=1, source_target_pairs={{0,24},{4,28},{8,0},{12,4},{16,8},{20,12},{24,16},{28,20},{1,25},{... | collective-permute-start | bytes 417800 | tf_op jit(solution)/shard_map/ppermute | solution.py:372
  21.2 14.5 %collective-permute-start.17 = (bf16[4,32,2176]{2,1,0:T(8,128)(2,1)S(1)}, bf16[4,32,2176]{2,1,0:T(8,128)(2,1)S(1)}, u32[]{:S(2)}, u32[]{:S(2)}) collective-permute-start(bf16[4,32,2176]{2,1,0:T(8,128)(2,1)S(1)} %pad_maximum_fusion), channel_id=1, source_target_pairs={{0,4},{4,0},{8,12},{12,8},{16,20},{20,16},{24,28},{28,24},{1,5},{5... | collective-permute-start | bytes 1671176 | tf_op jit(solution)/shard_map/ppermute | solution.py:372
  35.8 25.6 %collective-permute-start.18 = (bf16[8,32,2176]{2,1,0:T(8,128)(2,1)S(1)}, bf16[8,32,2176]{2,1,0:T(8,128)(2,1)S(1)}, u32[]{:S(2)}, u32[]{:S(2)}) collective-permute-start(bf16[8,32,2176]{2,1,0:T(8,128)(2,1)S(1)} %get-tuple-element.32), channel_id=1, source_target_pairs={{0,2},{1,3},{2,0},{3,1},{4,6},{5,7},{6,4},{7,5},{8,10},{9,11},{10,... | collective-permute-start | bytes 3342344 | tf_op jit(solution)/shard_map/ppermute | solution.py:372
  61.6 41.9 %collective-permute-start.19 = (bf16[16,32,2176]{2,1,0:T(8,128)(2,1)S(1)}, bf16[16,32,2176]{2,1,0:T(8,128)(2,1)}, u32[]{:S(2)}, u32[]{:S(2)}) collective-permute-start(bf16[16,32,2176]{2,1,0:T(8,128)(2,1)S(1)} %constant_dynamic-update-slice_fusion.5.near_ref), channel_id=1, source_target_pairs={{0,1},{1,0},{2,3},{3,2},{4,5},{5,4},{6,7},{7,6},{8,9},{9,8},{10,11... | collective-permute-start | bytes 6684680 | tf_op jit(solution)/shard_map/ppermute | solution.py:372
  65.5 35.8 %collective-permute-start.10 = (bf16[192,768]{1,0:T(8,128)(2,1)}, bf16[192,768]{1,0:T(8,128)(2,1)}, u32[]{:S(2)}, u32[]{:S(2)}) collective-permute-start(bf16[192,768]{1,0:T(8,128)(2,1)} %get-tuple-element.18), channel_id=1, source_target_pairs={{0,16},{4,20},{8,24},{12,28},{16,0},{20,4},{24,8},{28,12},{1,17},{... | collective-permute-start | bytes 884744 | tf_op jit(solution)/shard_map/ppermute | solution.py:372
  68.2 33.7 %collective-permute-start.11 = (bf16[192,768]{1,0:T(8,128)(2,1)}, bf16[192,768]{1,0:T(8,128)(2,1)}, u32[]{:S(2)}, u32[]{:S(2)}) collective-permute-start(bf16[192,768]{1,0:T(8,128)(2,1)} %get-tuple-element.17), channel_id=1, source_target_pairs={{0,20},{4,24},{8,28},{12,0},{16,4},{20,8},{24,12},{28,16},{1,21},{... | collective-permute-start | bytes 884744 | tf_op jit(solution)/shard_map/ppermute | solution.py:372
  70.2 19.5 %collective-permute-start = (bf16[128,512]{1,0:T(8,128)(2,1)S(1)}, bf16[128,512]{1,0:T(8,128)(2,1)S(1)}, u32[]{:S(2)}, u32[]{:S(2)}) collective-permute-start(bf16[128,512]{1,0:T(8,128)(2,1)S(1)} %get-tuple-element.29), channel_id=1, source_target_pairs={{0,4},{4,8},{8,12},{12,16},{16,20},{20,24},{24,28},{28,0},{1,5},{5... | collective-permute-start | bytes 393224 | tf_op jit(solution)/shard_map/ppermute | solution.py:372
  73.9 25.4 %collective-permute-start.1 = (bf16[128,512]{1,0:T(8,128)(2,1)S(1)}, bf16[128,512]{1,0:T(8,128)(2,1)S(1)}, u32[]{:S(2)}, u32[]{:S(2)}) collective-permute-start(bf16[128,512]{1,0:T(8,128)(2,1)S(1)} %get-tuple-element.28), channel_id=1, source_target_pairs={{0,8},{4,12},{8,16},{12,20},{16,24},{20,28},{24,0},{28,4},{1,9},{5... | collective-permute-start | bytes 393224 | tf_op jit(solution)/shard_map/ppermute | solution.py:372
  89.7 50.9 %copy-start.12 = (bf16[128,512]{1,0:T(8,128)(2,1)}, bf16[128,512]{1,0:T(8,128)(2,1)S(1)}, u32[]{:S(2)}) copy-start(bf16[128,512]{1,0:T(8,128)(2,1)S(1)} %collective-permute-done.refs_1_) | copy-start | bytes 393220
  89.7 50.9 %collective-permute-start.12 = (bf16[192,768]{1,0:T(8,128)(2,1)}, bf16[192,768]{1,0:T(8,128)(2,1)S(1)}, u32[]{:S(2)}, u32[]{:S(2)}) collective-permute-start(bf16[192,768]{1,0:T(8,128)(2,1)} %get-tuple-element.23), channel_id=1, source_target_pairs={{0,24},{4,28},{8,0},{12,4},{16,8},{20,12},{24,16},{28,20},{1,25},{... | collective-permute-start | bytes 884744 | tf_op jit(solution)/shard_map/ppermute | solution.py:372
  99.9 41.5 %collective-permute-start.13 = (bf16[192,768]{1,0:T(8,128)(2,1)}, bf16[192,768]{1,0:T(8,128)(2,1)S(1)}, u32[]{:S(2)}, u32[]{:S(2)}) collective-permute-start(bf16[192,768]{1,0:T(8,128)(2,1)} %get-tuple-element.16), channel_id=1, source_target_pairs={{0,28},{4,0},{8,4},{12,8},{16,12},{20,16},{24,20},{28,24},{1,29},{... | collective-permute-start | bytes 884744 | tf_op jit(solution)/shard_map/ppermute | solution.py:372
  101.3 41.1 %collective-permute-start.7 = (bf16[192,768]{1,0:T(8,128)(2,1)}, bf16[192,768]{1,0:T(8,128)(2,1)S(1)}, u32[]{:S(2)}, u32[]{:S(2)}) collective-permute-start(bf16[192,768]{1,0:T(8,128)(2,1)} %get-tuple-element.21), channel_id=1, source_target_pairs={{0,4},{4,8},{8,12},{12,16},{16,20},{20,24},{24,28},{28,0},{1,5},{5... | collective-permute-start | bytes 884744 | tf_op jit(solution)/shard_map/ppermute | solution.py:372
  101.9 42.8 %collective-permute-start.8 = (bf16[192,768]{1,0:T(8,128)(2,1)}, bf16[192,768]{1,0:T(8,128)(2,1)}, u32[]{:S(2)}, u32[]{:S(2)}) collective-permute-start(bf16[192,768]{1,0:T(8,128)(2,1)} %get-tuple-element.20), channel_id=1, source_target_pairs={{0,8},{4,12},{8,16},{12,20},{16,24},{20,28},{24,0},{28,4},{1,9},{5... | collective-permute-start | bytes 884744 | tf_op jit(solution)/shard_map/ppermute | solution.py:372
  103.5 44.2 %collective-permute-start.9 = (bf16[192,768]{1,0:T(8,128)(2,1)}, bf16[192,768]{1,0:T(8,128)(2,1)S(1)}, u32[]{:S(2)}, u32[]{:S(2)}) collective-permute-start(bf16[192,768]{1,0:T(8,128)(2,1)} %get-tuple-element.19), channel_id=1, source_target_pairs={{0,12},{4,16},{8,20},{12,24},{16,28},{20,0},{24,4},{28,8},{1,13},{... | collective-permute-start | bytes 884744 | tf_op jit(solution)/shard_map/ppermute | solution.py:372
  107.5 25.2 %all-to-all-start = ((f32[8,1,768]{2,1,0:T(1,128)}), f32[8,1,768]{2,1,0:T(1,128)S(1)}, u32[]{:S(2)}, u32[]{:S(2)}) async-start(f32[8,1,768]{2,1,0:T(1,128)} %bitcast.74), calls=%async_computation | async-start | bytes 49152 | tf_op jit(solution)/shard_map/all_to_all | solution.py:405
  133.3 8.1 %copy-start.4 = (bf16[128,512]{1,0:T(8,128)(2,1)S(1)}, bf16[128,512]{1,0:T(8,128)(2,1)}, u32[]{:S(2)}) copy-start(bf16[128,512]{1,0:T(8,128)(2,1)} %get-tuple-element.26) | copy-start | bytes 393220
  133.3 9.1 %copy-start.3 = (bf16[128,512]{1,0:T(8,128)(2,1)S(1)}, bf16[128,512]{1,0:T(8,128)(2,1)}, u32[]{:S(2)}) copy-start(bf16[128,512]{1,0:T(8,128)(2,1)} %get-tuple-element.25) | copy-start | bytes 393220
  140.7 8.5 %copy-start.8 = (bf16[192,768]{1,0:T(8,128)(2,1)}, bf16[192,768]{1,0:T(8,128)(2,1)S(1)}, u32[]{:S(2)}) copy-start(bf16[192,768]{1,0:T(8,128)(2,1)S(1)} %collective-permute-done.12.refs_6_) | copy-start | bytes 884740
  140.7 17.4 %collective-permute-start.2 = (bf16[128,512]{1,0:T(8,128)(2,1)S(1)}, bf16[128,512]{1,0:T(8,128)(2,1)S(1)}, u32[]{:S(2)}, u32[]{:S(2)}) collective-permute-start(bf16[128,512]{1,0:T(8,128)(2,1)S(1)} %copy-done.5), channel_id=1, source_target_pairs={{0,12},{4,16},{8,20},{12,24},{16,28},{20,0},{24,4},{28,8},{1,13},{... | collective-permute-start | bytes 393224 | tf_op jit(solution)/shard_map/ppermute | solution.py:372
  141.4 16.7 %collective-permute-start.3 = (bf16[128,512]{1,0:T(8,128)(2,1)S(1)}, bf16[128,512]{1,0:T(8,128)(2,1)S(1)}, u32[]{:S(2)}, u32[]{:S(2)}) collective-permute-start(bf16[128,512]{1,0:T(8,128)(2,1)S(1)} %copy-done.4), channel_id=1, source_target_pairs={{0,16},{4,20},{8,24},{12,28},{16,0},{20,4},{24,8},{28,12},{1,17},{... | collective-permute-start | bytes 393224 | tf_op jit(solution)/shard_map/ppermute | solution.py:372
  142.3 15.8 %collective-permute-start.4 = (bf16[128,512]{1,0:T(8,128)(2,1)S(1)}, bf16[128,512]{1,0:T(8,128)(2,1)S(1)}, u32[]{:S(2)}, u32[]{:S(2)}) collective-permute-start(bf16[128,512]{1,0:T(8,128)(2,1)S(1)} %copy-done.3), channel_id=1, source_target_pairs={{0,20},{4,24},{8,28},{12,0},{16,4},{20,8},{24,12},{28,16},{1,21},{... | collective-permute-start | bytes 393224 | tf_op jit(solution)/shard_map/ppermute | solution.py:372
  144.7 13.4 %collective-permute-start.5 = (bf16[128,512]{1,0:T(8,128)(2,1)S(1)}, bf16[128,512]{1,0:T(8,128)(2,1)S(1)}, u32[]{:S(2)}, u32[]{:S(2)}) collective-permute-start(bf16[128,512]{1,0:T(8,128)(2,1)S(1)} %get-tuple-element.31), channel_id=1, source_target_pairs={{0,24},{4,28},{8,0},{12,4},{16,8},{20,12},{24,16},{28,20},{1,25},{... | collective-permute-start | bytes 393224 | tf_op jit(solution)/shard_map/ppermute | solution.py:372
  147.7 10.5 %collective-permute-start.6 = (bf16[128,512]{1,0:T(8,128)(2,1)S(1)}, bf16[128,512]{1,0:T(8,128)(2,1)S(1)}, u32[]{:S(2)}, u32[]{:S(2)}) collective-permute-start(bf16[128,512]{1,0:T(8,128)(2,1)S(1)} %get-tuple-element.24), channel_id=1, source_target_pairs={{0,28},{4,0},{8,4},{12,8},{16,12},{20,16},{24,20},{28,24},{1,29},{... | collective-permute-start | bytes 393224 | tf_op jit(solution)/shard_map/ppermute | solution.py:372
  158.9 28.5 %copy-start.7 = (f32[1,1536]{1,0:T(1,128)S(1)}, f32[1,1536]{1,0:T(1,128)}, u32[]{:S(2)}) copy-start(f32[1,1536]{1,0:T(1,128)} %bias_ref.1) | copy-start | bytes 18436
  158.9 37.6 %copy-start = (bf16[128,1536]{1,0:T(8,128)(2,1)S(1)}, bf16[128,1536]{1,0:T(8,128)(2,1)}, u32[]{:S(2)}) copy-start(bf16[128,1536]{1,0:T(8,128)(2,1)} %lat_ref.1) | copy-start | bytes 1179652
  158.9 40.6 %copy-start.6 = (f32[1536]{0:T(1024)S(1)}, f32[1536]{0:T(1024)}, u32[]{:S(2)}) copy-start(f32[1536]{0:T(1024)} %param.13) | copy-start | bytes 18436
  179.9 14.7 %all-to-all-start.1 = ((f32[8,24,128]{2,1,0:T(8,128)}), f32[8,24,128]{2,1,0:T(8,128)S(1)}, u32[]{:S(2)}, u32[]{:S(2)}) async-start(f32[8,24,128]{2,1,0:T(8,128)} %shard_map.125), calls=%async_computation.1 | async-start | bytes 196608 | tf_op jit(solution)/shard_map/all_to_all | solution.py:500
  194.6 2.8 %collective-permute-start.20 = (f32[13,128]{1,0:T(8,128)S(1)}, f32[13,128]{1,0:T(8,128)S(1)}, u32[]{:S(2)}, u32[]{:S(2)}) collective-permute-start(f32[13,128]{1,0:T(8,128)S(1)} %slice_reduce_fusion), channel_id=1, source_target_pairs={{0,1},{1,0},{2,3},{3,2},{4,5},{5,4},{6,7},{7,6},{8,9},{9,8},{10,11... | collective-permute-start | bytes 19976 | tf_op jit(solution)/shard_map/ppermute | solution.py:506
  194.7 3.7 %collective-permute-start.21 = (f32[13,128]{1,0:T(8,128)S(1)}, f32[13,128]{1,0:T(8,128)S(1)}, u32[]{:S(2)}, u32[]{:S(2)}) collective-permute-start(f32[13,128]{1,0:T(8,128)S(1)} %slice_reduce_fusion), channel_id=1, source_target_pairs={{0,2},{1,3},{2,0},{3,1},{4,6},{5,7},{6,4},{7,5},{8,10},{9,11},{10,... | collective-permute-start | bytes 19976 | tf_op jit(solution)/shard_map/ppermute | solution.py:506
  196.3 3.1 %collective-permute-start.22 = (f32[13,128]{1,0:T(8,128)S(1)}, f32[13,128]{1,0:T(8,128)S(1)}, u32[]{:S(2)}, u32[]{:S(2)}) collective-permute-start(f32[13,128]{1,0:T(8,128)S(1)} %slice_reduce_fusion), channel_id=1, source_target_pairs={{0,3},{1,2},{2,1},{3,0},{4,7},{5,6},{6,5},{7,4},{8,11},{9,10},{10,... | collective-permute-start | bytes 19976 | tf_op jit(solution)/shard_map/ppermute | solution.py:506
  (12 other events, 39.3 us)
where the time goes:
time: 201 us; the launch traced here: 200 us
  waiting for transfers between devices  89.3 us (44%)
  starting transfers between devices  56.1 us (28%)
  Pallas kernels  39 us (19%)
  local copies, waits for them, and re-layouts  13.1 us (7%)
    ppermute x20, waiting for transfers between devices, send(): return lax.ppermute(array, axis, [(i, target(i)) for i in range(size)])  59.8 us
    ppermute x20, starting transfers between devices, send(): return lax.ppermute(array, axis, [(i, target(i)) for i in range(size)])  43.3 us
    pallas_call x1, Pallas kernels, spread(): pl.pallas_call(attend_kernel, out_shape=jax.ShapeDtypeStruct((ring, slots...  21 us
    all_to_all x1, waiting for transfers between devices, spread(): lax.all_to_all(steer.reshape(ring, columns), 'ctx', 0, 0, tiled=True)  20.4 us
    pallas_call x1, Pallas kernels, spread(): pl.pallas_call(query_kernel, out_shape=(jax.ShapeDtypeStruct((queries, co...  8.87 us
    all_to_all x1, starting transfers between devices, spread(): arrived = lax.all_to_all(sums, 'ctx', 0, 0, tiled=True)  7.53 us
    pallas_call x1, Pallas kernels, spread(): pl.pallas_call(keys_kernel, out_shape=(jax.ShapeDtypeStruct((queries, ql)...  7.4 us
    all_to_all x1, waiting for transfers between devices, spread(): arrived = lax.all_to_all(sums, 'ctx', 0, 0, tiled=True)  7.09 us
  transfers between devices with their start and end apart: 25, of which 9 were waited for; matrix products, arithmetic and copies ran while one was open for 4% of the time, Pallas kernels for 8%

commit v1 on v0

--- a/solution.py
+++ b/solution.py
@@ -195,11 +195,13 @@
 
 
 def query_kernel(place, *refs):
-    count = len(refs) - 5
-    weights, (c_ref, steer_ref, q_ref, proj_ref, full_ref) = refs[:count], refs[count:]
+    count = (len(refs) - 5) // 2
+    weights, steers = refs[:count], refs[count : 2 * count]
+    c_ref, q_ref, proj_ref, full_ref, steer_ref = refs[2 * count :]
     depth = weights[0].shape[0]
-    for index, ref in enumerate(weights):
-        full_ref[pl.ds(pl.multiple_of(place[index] * depth, 64), depth), :] = ref[...]
+    for index in range(count):
+        full_ref[pl.ds(pl.multiple_of(place[index] * depth, 64), depth), :] = weights[index][...]
+        steer_ref[pl.ds(place[index], 1), :] = steers[index][...]
     step = 256
     for start in range(0, c_ref.shape[0], step):
         projected = dot(c_ref[start : start + step, :], full_ref[...])
@@ -212,20 +214,7 @@
             ).astype(bf16)
 
 
-def attend_kernel(mask, place, *refs):
-    count = len(refs) - 17
-    cots = refs[:count]
-    (
-        q_ref, proj_ref, tail_ref, wide_ref, value_ref, weight_ref, out_ref,
-        cot_ref, sums_ref, weighted_ref, row_ref, score_ref, dot_ref, first_ref, second_ref, grad_ref, pair_ref,
-    ) = refs[count:]
-    nblocks = count
-    heads = wide_ref.shape[0]
-    width = NOPE + ROPE
-    scale = width ** (-0.5)
-    for index, ref in enumerate(cots):
-        cot_ref[place[index]] = ref[...]
-
+def list_pairs(mask, pair_ref, nblocks):
     def list_step(index, found):
         block, key = index // mask.shape[1], index % mask.shape[1]
         pair_ref[0, found] = block
@@ -235,86 +224,137 @@
     found = lax.fori_loop(0, nblocks * mask.shape[1], list_step, 0)
     pair_ref[0, found] = nblocks
     pair_ref[1, found] = 0
-    trips = (found + UNROLL - 1) // UNROLL
-
-    def each_pair(visit):
-        def trip(index, carry):
-            for part in range(UNROLL):
-                pair = index * UNROLL + part
-                visit(pair, pair_ref[0, pair], pair_ref[1, pair])
-            return carry
-
-        lax.fori_loop(0, trips, trip, 0)
-
-    def each_block(visit):
-        def trip(block, carry):
-            visit(block)
-            return carry
-
-        lax.fori_loop(0, nblocks, trip, 0)
-
-    def span(block):
-        return pl.ds(pl.multiple_of(block * BLK, BLK), BLK)
-
-    first_ref[...] = jnp.full_like(first_ref, lowest)
+    return found
+
+
+def each_pair(found, pair_ref, visit):
+    def trip(index, carry):
+        for part in range(UNROLL):
+            pair = index * UNROLL + part
+            visit(pair, pair_ref[0, pair], pair_ref[1, pair])
+        return carry
+
+    lax.fori_loop(0, (found + UNROLL - 1) // UNROLL, trip, 0)
+
+
+def each(count, visit):
+    def trip(index, carry):
+        visit(index)
+        return carry
+
+    lax.fori_loop(0, count, trip, 0)
+
+
+def span(block):
+    return pl.ds(pl.multiple_of(block * BLK, BLK), BLK)
+
+
+def window(head):
+    left = head // 2 * 2 * (NOPE + ROPE) + head % 2 * NOPE
+    return slice(left, left + WIDE)
+
+
+def weights_kernel(mask, q_ref, wide_ref, out_ref, score_ref, sum_ref, peak_ref, pair_ref, sems):
+    nblocks = mask.shape[0]
+    heads = wide_ref.shape[0]
+    scale = (NOPE + ROPE) ** (-0.5)
+    found = list_pairs(mask, pair_ref, nblocks)
+    sum_ref[...] = jnp.full_like(sum_ref, lowest)
 
     def score(pair, block, key):
         rows = span(jnp.minimum(block, nblocks - 1))
         for head in range(heads):
-            left = head // 2 * 2 * width + head % 2 * NOPE
-            scores = contract_last(q_ref[rows, left : left + WIDE], wide_ref[head, span(key), :]) * scale
+            scores = contract_last(q_ref[rows, window(head)], wide_ref[head, span(key), :]) * scale
             score_ref[pair, head] = scores
-            first_ref[block, head] = jnp.maximum(first_ref[block, head], scores)
-
-    each_pair(score)
-
-    peak_ref = grad_ref
+            sum_ref[block, head] = jnp.maximum(sum_ref[block, head], scores)
+
+    each_pair(found, pair_ref, score)
 
     def find_peak(block):
         for head in range(heads):
-            peak = jnp.max(first_ref[block, head], axis=1, keepdims=True)
-            peak_ref[block, :, head * BLK : (head + 1) * BLK] = jnp.broadcast_to(peak, (BLK, BLK))
-
-    each_block(find_peak)
-    peak_ref[nblocks] = jnp.zeros_like(peak_ref[nblocks])
-    first_ref[...] = jnp.zeros_like(first_ref)
-    second_ref[...] = jnp.zeros_like(second_ref)
+            peak = jnp.max(sum_ref[block, head], axis=1, keepdims=True)
+            peak_ref[block, head] = jnp.broadcast_to(peak, (BLK, BLK))
+            sum_ref[block, head] = jnp.zeros((BLK, BLK), f32)
+
+    each(nblocks + 1, find_peak)
+
+    def weigh(pair, block, key):
+        for head in range(heads):
+            weights = jnp.exp(score_ref[pair, head] - peak_ref[block, head])
+            score_ref[pair, head] = weights
+            sum_ref[block, head] = sum_ref[block, head] + weights
+
+    each_pair(found, pair_ref, weigh)
+
+    def invert(block):
+        for head in range(heads):
+            total = jnp.sum(sum_ref[block, head], axis=1, keepdims=True)
+            peak_ref[block, head] = jnp.broadcast_to(1.0 / total, (BLK, BLK))
+
+    each(nblocks, invert)
+
+    def copy(pair):
+        return pltpu.make_async_copy(score_ref.at[pair], out_ref.at[pair], sems.at[pair])
+
+    def finish(pair):
+        block = pair_ref[0, pair]
+        for head in range(heads):
+            score_ref[pair, head] = score_ref[pair, head] * peak_ref[block, head]
+        copy(pair).start()
+
+    each(found, finish)
+    each(found, lambda pair: copy(pair).wait())
+
+
+def slope_kernel(mask, place, *refs):
+    count = len(refs) - 17
+    cots = refs[:count]
+    (
+        held_ref, proj_ref, tail_ref, wide_ref, value_ref, weight_ref, out_ref,
+        cot_ref, sums_ref, weighted_ref, row_ref, prob_ref, dot_ref, mean_ref, grad_ref, pair_ref, sems,
+    ) = refs[count:]
+    nblocks = count
+    heads = wide_ref.shape[0]
+    scale = (NOPE + ROPE) ** (-0.5)
+    found = list_pairs(mask, pair_ref, nblocks)
+
+    def copy(pair):
+        return pltpu.make_async_copy(held_ref.at[pair], prob_ref.at[pair], sems.at[pair])
+
+    each(found, lambda pair: copy(pair).start())
+    for index, ref in enumerate(cots):
+        cot_ref[place[index]] = ref[...]
+    mean_ref[...] = jnp.zeros_like(mean_ref)
+    grad_ref[...] = jnp.zeros_like(grad_ref)
+    each(found, lambda pair: copy(pair).wait())
 
     def weigh(pair, block, key):
         source = jnp.minimum(block, nblocks - 1)
         for head in range(heads):
             lanes = slice(head * VD, (head + 1) * VD)
             dots = contract_last(cot_ref[source, :, lanes], value_ref[span(key), lanes])
-            weights = jnp.exp(score_ref[pair, head] - peak_ref[block, :, head * BLK : (head + 1) * BLK])
-            score_ref[pair, head] = weights
             dot_ref[pair, head] = dots
-            first_ref[block, head] = first_ref[block, head] + weights
-            second_ref[block, head] = second_ref[block, head] + weights * dots
-
-    each_pair(weigh)
-
-    def normalise(block):
-        for head in range(heads):
-            total = jnp.sum(first_ref[block, head], axis=1, keepdims=True)
-            mixed = jnp.sum(second_ref[block, head], axis=1, keepdims=True)
-            first_ref[block, head] = jnp.broadcast_to(scale / total, (BLK, BLK))
-            second_ref[block, head] = jnp.broadcast_to(mixed / total, (BLK, BLK))
-
-    each_block(normalise)
-    grad_ref[...] = jnp.zeros_like(grad_ref)
+            mean_ref[block, head] = mean_ref[block, head] + prob_ref[pair, head] * dots
+
+    each_pair(found, pair_ref, weigh)
+
+    def average(block):
+        for head in range(heads):
+            mean = jnp.sum(mean_ref[block, head], axis=1, keepdims=True)
+            mean_ref[block, head] = jnp.broadcast_to(mean, (BLK, BLK))
+
+    each(nblocks, average)
 
     def gather(pair, block, key):
         for head in range(heads):
-            left = head // 2 * 2 * width + head % 2 * NOPE
-            slope = score_ref[pair, head] * (dot_ref[pair, head] - second_ref[block, head])
-            slope = (slope * first_ref[block, head]).astype(bf16)
-            lanes = slice(left, left + WIDE)
-            grad_ref[block, :, lanes] = grad_ref[block, :, lanes] + dot(slope, wide_ref[head, span(key), :])
-
-    each_pair(gather)
+            slope = prob_ref[pair, head] * (dot_ref[pair, head] - mean_ref[block, head])
+            gained = dot(slope.astype(bf16), wide_ref[head, span(key), :])
+            grad_ref[block, :, window(head)] = grad_ref[block, :, window(head)] + gained
+
+    each_pair(found, pair_ref, gather)
 
     def reduce(block):
-        grad = grad_ref[block]
+        grad = grad_ref[block] * scale
         tail = tail_ref[span(block), :].astype(f32)
         inv = tail[:, ROPE : ROPE + 1] + tail[:, ROPE + 1 : ROPE + 2]
         sums_ref[pl.ds(block, 1), :] = jnp.sum(grad, axis=0, keepdims=True)
@@ -325,7 +365,7 @@
             narrow = narrow + products[:, start : start + 128]
         row_ref[pl.ds(block, 1), :] = jnp.sum(narrow.T, axis=0, keepdims=True)
 
-    each_block(reduce)
+    each(nblocks, reduce)
     weighted = weighted_ref[...]
     high = weighted.astype(bf16)
     low = (weighted - high.astype(f32)).astype(bf16)
@@ -402,7 +442,7 @@
     near = jnp.concatenate([both, other])
     far = send(near, "head", lambda i: i ^ 1, head_shards)
     cot_parts = [chunk(d_out, cot_columns, 0)] + [turn(chunk(d_out, cot_columns, step), step) for step in shifts]
-    all_steer = lax.all_to_all(steer.reshape(ring, columns), "ctx", 0, 0, tiled=True)
+    steer_parts = [chunk(steer, columns, 0)] + [turn(chunk(steer, columns, step), step) for step in shifts]
 
     z, x = mine // 2, mine % 2
     places = []
@@ -454,25 +494,46 @@
         grid_spec=pltpu.PrefetchScalarGridSpec(
             num_scalar_prefetch=1,
             grid=(1,),
-            in_specs=[full(weight_parts[0].shape)] * ring + [full((queries, ql)), full((ring, columns))],
+            in_specs=[full(weight_parts[0].shape)] * ring + [full((1, columns))] * ring + [full((queries, ql))],
             out_specs=(full((queries, columns)), full((queries, columns)), full((ql, columns))),
+            scratch_shapes=[pltpu.VMEM((ring, columns), f32)],
         ),
         compiler_params=params(),
         cost_estimate=cost(3 * 10**9, 10**7),
-    )(sources, *weight_parts, c_query, all_steer)
+    )(sources, *weight_parts, *steer_parts, c_query)
 
     used = (ql + BLK + columns) // 128
     slots = (used + 7) // 8 * 8
     pairs = (ring * ring + UNROLL - 1) // UNROLL * UNROLL
+    tiles = (pairs, heads, BLK, BLK)
+    held = pl.pallas_call(
+        weights_kernel,
+        out_shape=jax.ShapeDtypeStruct(tiles, f32),
+        grid_spec=pltpu.PrefetchScalarGridSpec(
+            num_scalar_prefetch=1,
+            grid=(1,),
+            in_specs=[full((queries, columns)), full((heads, queries, WIDE))],
+            out_specs=pl.BlockSpec(memory_space=pl.ANY),
+            scratch_shapes=[
+                pltpu.VMEM(tiles, f32),
+                pltpu.VMEM((ring + 1, heads, BLK, BLK), f32),
+                pltpu.VMEM((ring + 1, heads, BLK, BLK), f32),
+                pltpu.SMEM((2, pairs + UNROLL), jnp.int32),
+                pltpu.SemaphoreType.DMA((pairs,)),
+            ],
+        ),
+        compiler_params=params(),
+        cost_estimate=cost(2 * 10**9, 10**7),
+    )(block_mask, query, wide)
     sums = pl.pallas_call(
-        attend_kernel,
+        slope_kernel,
         out_shape=jax.ShapeDtypeStruct((ring, slots, 128), f32),
         grid_spec=pltpu.PrefetchScalarGridSpec(
             num_scalar_prefetch=2,
             grid=(1,),
             in_specs=[full((BLK, cot_columns))] * ring
             + [
-                full((queries, columns)),
+                pl.BlockSpec(memory_space=pl.ANY),
                 full((queries, columns)),
                 full((queries, 2 * ROPE)),
                 full((heads, queries, WIDE)),
@@ -485,17 +546,17 @@
                 pltpu.VMEM((ring, columns), f32),
                 pltpu.VMEM((ring, columns), f32),
                 pltpu.VMEM((ring, BLK), f32),
-                pltpu.VMEM((pairs, heads, BLK, BLK), f32),
-                pltpu.VMEM((pairs, heads, BLK, BLK), f32),
-                pltpu.VMEM((ring + 1, heads, BLK, BLK), f32),
+                pltpu.VMEM(tiles, f32),
+                pltpu.VMEM(tiles, f32),
                 pltpu.VMEM((ring + 1, heads, BLK, BLK), f32),
                 pltpu.VMEM((ring + 1, BLK, columns), f32),
                 pltpu.SMEM((2, pairs + UNROLL), jnp.int32),
+                pltpu.SemaphoreType.DMA((pairs,)),
             ],
         ),
         compiler_params=params(),
-        cost_estimate=cost(8 * 10**9, 10**7),
-    )(block_mask, sources, *cot_parts, query, projected, tail, wide, values, weight)
+        cost_estimate=cost(4 * 10**9, 10**7),
+    )(block_mask, sources, *cot_parts, held, projected, tail, wide, values, weight)
 
     arrived = lax.all_to_all(sums, "ctx", 0, 0, tiled=True)
     cut = (ql + BLK) // 128

time: 201 us -> 208 us (1.035)
  Pallas kernels: 39 us -> 47.3 us
  starting transfers between devices: 56.1 us -> 52.9 us
  waiting for transfers between devices: 89.3 us -> 91.5 us
    ppermute x20 -> x27, waiting for transfers between devices: 59.8 us -> 82.5 us  [send(): return lax.ppermute(array, axis, [(i, target(i)) for i in range(size)])]
    all_to_all x1 -> x0, waiting for transfers between devices: 20.4 us -> none  [spread(): lax.all_to_all(steer.reshape(ring, columns), 'ctx', 0, 0, tiled=True)]
    pallas_call x1 -> x2, Pallas kernels: 21 us -> 29.1 us  [the longest x1 17.4 us: spread(): pl.pallas_call(slope_kernel, out_shape=jax.ShapeDtypeStruct((ring, slots,...]
    all_to_all x1 -> x0, starting transfers between devices: 3.34 us -> none  [spread(): lax.all_to_all(steer.reshape(ring, columns), 'ctx', 0, 0, tiled=True)]
    ppermute x20 -> x27, starting transfers between devices: 43.3 us -> 45.7 us  [send(): return lax.ppermute(array, axis, [(i, target(i)) for i in range(size)])]
    all_to_all x1, starting transfers between devices: 7.53 us -> 5.34 us  [spread(): arrived = lax.all_to_all(sums, 'ctx', 0, 0, tiled=True)]
    unnamed x44 -> x51, local copies, waits for them, and re-layouts: 4.53 us -> 4.03 us
    dynamic_slice x2 -> x3, local copies, waits for them, and re-layouts: 4.54 us -> 5.01 us  [chunk(): lax.dynamic_slice_in_dim(array, (mine + step) % ring * width, width, 1)]
  transfers between devices with their start and end apart: 25 -> 31, of which waited for: 9 -> 12; matrix products, arithmetic and copies ran while one was open for 4% -> 4% of each run, Pallas kernels for 8% -> 14%
where the time goes in v1:
time: 208 us; the launch traced here: 207 us
  waiting for transfers between devices  91.5 us (44%)
  starting transfers between devices  52.9 us (25%)
  Pallas kernels  47.3 us (23%)
  local copies, waits for them, and re-layouts  13.2 us (6%)
    ppermute x27, waiting for transfers between devices, send(): return lax.ppermute(array, axis, [(i, target(i)) for i in range(size)])  82.5 us
    ppermute x27, starting transfers between devices, send(): return lax.ppermute(array, axis, [(i, target(i)) for i in range(size)])  45.7 us
    pallas_call x1, Pallas kernels, spread(): pl.pallas_call(slope_kernel, out_shape=jax.ShapeDtypeStruct((ring, slots,...  17.4 us
    pallas_call x1, Pallas kernels, spread(): pl.pallas_call(weights_kernel, out_shape=jax.ShapeDtypeStruct(tiles, f32)...  11.7 us
    pallas_call x1, Pallas kernels, spread(): pl.pallas_call(query_kernel, out_shape=(jax.ShapeDtypeStruct((queries, co...  9.12 us
    pallas_call x1, Pallas kernels, spread(): pl.pallas_call(keys_kernel, out_shape=(jax.ShapeDtypeStruct((queries, ql)...  7.29 us
    all_to_all x1, waiting for transfers between devices, spread(): arrived = lax.all_to_all(sums, 'ctx', 0, 0, tiled=True)  7.09 us
    all_to_all x1, starting transfers between devices, spread(): arrived = lax.all_to_all(sums, 'ctx', 0, 0, tiled=True)  5.34 us
  transfers between devices with their start and end apart: 31, of which 12 were waited for; matrix products, arithmetic and copies ran while one was open for 4% of the time, Pallas kernels for 14%

profile of v1, /device:TPU:0, one launch (start us, length us, event | category | flops | bytes accessed | tf_op | source)
XLA Modules:
  0.0 207.4 jit_solution(14454471220699182220)
XLA Ops:
  0.6 1.4 copy.14.rope_ref
  2.1 1.3 broadcast_in_dim.13.gain_ref
  3.4 1.8 shard_map.122
  5.1 3.1 %collective-permute-start.21 = (bf16[32,2176]{1,0:T(8,128)(2,1)}, bf16[32,2176]{1,0:T(8,128)(2,1)S(1)}, u32[]{:S(2)}, u32[]{:S(2)}) collective-permute-start(bf16[32,2176]{1,0:T(8,128)(2,1)} %shard_map.122), channel_id=1, source_target_pairs={{0,8},{4,12},{8,16},{12,20},{16,24},{20,28},{24,0},{28,4},{1,9},{5... | collective-permute-start | bytes 417800 | tf_op jit(solution)/shard_map/ppermute | solution.py:412
  8.2 2.6 %collective-permute-start.22 = (bf16[32,2176]{1,0:T(8,128)(2,1)}, bf16[32,2176]{1,0:T(8,128)(2,1)S(1)}, u32[]{:S(2)}, u32[]{:S(2)}) collective-permute-start(bf16[32,2176]{1,0:T(8,128)(2,1)} %shard_map.122), channel_id=1, source_target_pairs={{0,16},{4,20},{8,24},{12,28},{16,0},{20,4},{24,8},{28,12},{1,17},{... | collective-permute-start | bytes 417800 | tf_op jit(solution)/shard_map/ppermute | solution.py:412
  10.8 1.3 collective-permute-start.23
  13.1 2.0 collective-permute-done.21
  15.0 5.1 %collective-permute-done.22 = bf16[32,2176]{1,0:T(8,128)(2,1)S(1)} collective-permute-done((bf16[32,2176]{1,0:T(8,128)(2,1)}, bf16[32,2176]{1,0:T(8,128)(2,1)S(1)}, u32[]{:S(2)}, u32[]{:S(2)}) %collective-permute-start.22) | collective-permute-done | bytes 139296 | tf_op jit(solution)/shard_map/ppermute | solution.py:412
  21.2 1.6 collective-permute-start.24
  22.8 12.9 %collective-permute-done.24 = bf16[4,32,2176]{2,1,0:T(8,128)(2,1)S(1)} collective-permute-done((bf16[4,32,2176]{2,1,0:T(8,128)(2,1)S(1)}, bf16[4,32,2176]{2,1,0:T(8,128)(2,1)S(1)}, u32[]{:S(2)}, u32[]{:S(2)}) %collective-permute-start.24) | collective-permute-done | bytes 557088 | tf_op jit(solution)/shard_map/ppermute | solution.py:412
  35.8 1.6 collective-permute-start.25
  37.4 24.0 %collective-permute-done.25 = bf16[8,32,2176]{2,1,0:T(8,128)(2,1)S(1)} collective-permute-done((bf16[8,32,2176]{2,1,0:T(8,128)(2,1)S(1)}, bf16[8,32,2176]{2,1,0:T(8,128)(2,1)S(1)}, u32[]{:S(2)}, u32[]{:S(2)}) %collective-permute-start.25) | collective-permute-done | bytes 1114144 | tf_op jit(solution)/shard_map/ppermute | solution.py:412
  61.8 3.7 %constant_dynamic-slice_fusion.8 = (bf16[192,768]{1,0:T(8,128)(2,1)}, bf16[192,768]{1,0:T(8,128)(2,1)}, bf16[192,768]{1,0:T(8,128)(2,1)}, bf16[192,768]{1,0:T(8,...) fusion(bf16[192,6144]{1,0:T(8,128)(2,1)} %param.14, ...), kind=kLoop, calls=%fused_computation.28 | loop fusion | bytes 4718624 | tf_op jit(solution)/shard_map/dynamic_slice | solution.py:409
  65.5 2.8 %collective-permute-start.10 = (bf16[192,768]{1,0:T(8,128)(2,1)}, bf16[192,768]{1,0:T(8,128)(2,1)}, u32[]{:S(2)}, u32[]{:S(2)}) collective-permute-start(bf16[192,768]{1,0:T(8,128)(2,1)} %get-tuple-element.18), channel_id=1, source_target_pairs={{0,16},{4,20},{8,24},{12,28},{16,0},{20,4},{24,8},{28,12},{1,17},{... | collective-permute-start | bytes 884744 | tf_op jit(solution)/shard_map/ppermute | solution.py:412
  70.0 3.6 %collective-permute-start.14 = (f32[1,768]{1,0:T(1,128)S(1)}, f32[1,768]{1,0:T(1,128)S(1)}, u32[]{:S(2)}, u32[]{:S(2)}) collective-permute-start(f32[1,768]{1,0:T(1,128)S(1)} %get-tuple-element.47), channel_id=1, source_target_pairs={{0,4},{4,8},{8,12},{12,16},{16,20},{20,24},{24,28},{28,0},{1,5},{5... | collective-permute-start | bytes 9224 | tf_op jit(solution)/shard_map/ppermute | solution.py:412
  73.6 12.3 %collective-permute-done.14.refs_9_ = f32[1,768]{1,0:T(1,128)S(1)} collective-permute-done((f32[1,768]{1,0:T(1,128)S(1)}, f32[1,768]{1,0:T(1,128)S(1)}, u32[]{:S(2)}, u32[]{:S(2)}) %collective-permute-start.14) | collective-permute-done | bytes 3104 | tf_op jit(solution)/shard_map/ppermute | solution.py:412
  85.9 3.7 %collective-permute-start.16 = (f32[1,768]{1,0:T(1,128)S(1)}, f32[1,768]{1,0:T(1,128)S(1)}, u32[]{:S(2)}, u32[]{:S(2)}) collective-permute-start(f32[1,768]{1,0:T(1,128)S(1)} %get-tuple-element.45), channel_id=1, source_target_pairs={{0,12},{4,16},{8,20},{12,24},{16,28},{20,0},{24,4},{28,8},{1,13},{... | collective-permute-start | bytes 9224 | tf_op jit(solution)/shard_map/ppermute | solution.py:412
  89.7 7.2 %collective-permute-start.17 = (f32[1,768]{1,0:T(1,128)S(1)}, f32[1,768]{1,0:T(1,128)S(1)}, u32[]{:S(2)}, u32[]{:S(2)}) collective-permute-start(f32[1,768]{1,0:T(1,128)S(1)} %get-tuple-element.44), channel_id=1, source_target_pairs={{0,16},{4,20},{8,24},{12,28},{16,0},{20,4},{24,8},{28,12},{1,17},{... | collective-permute-start | bytes 9224 | tf_op jit(solution)/shard_map/ppermute | solution.py:412
  99.0 2.4 %collective-permute-done.18.refs_13_ = f32[1,768]{1,0:T(1,128)S(1)} collective-permute-done((f32[1,768]{1,0:T(1,128)S(1)}, f32[1,768]{1,0:T(1,128)S(1)}, u32[]{:S(2)}, u32[]{:S(2)}) %collective-permute-start.18) | collective-permute-done | bytes 3104 | tf_op jit(solution)/shard_map/ppermute | solution.py:412
  102.7 3.3 %collective-permute-start.12 = (bf16[192,768]{1,0:T(8,128)(2,1)}, bf16[192,768]{1,0:T(8,128)(2,1)S(1)}, u32[]{:S(2)}, u32[]{:S(2)}) collective-permute-start(bf16[192,768]{1,0:T(8,128)(2,1)} %get-tuple-element.23), channel_id=1, source_target_pairs={{0,24},{4,28},{8,0},{12,4},{16,8},{20,12},{24,16},{28,20},{1,25},{... | collective-permute-start | bytes 884744 | tf_op jit(solution)/shard_map/ppermute | solution.py:412
  106.0 1.7 collective-permute-start.13
  108.6 2.7 %collective-permute-start.9 = (bf16[192,768]{1,0:T(8,128)(2,1)}, bf16[192,768]{1,0:T(8,128)(2,1)S(1)}, u32[]{:S(2)}, u32[]{:S(2)}) collective-permute-start(bf16[192,768]{1,0:T(8,128)(2,1)} %get-tuple-element.19), channel_id=1, source_target_pairs={{0,12},{4,16},{8,20},{12,24},{16,28},{20,0},{24,4},{28,8},{1,13},{... | collective-permute-start | bytes 884744 | tf_op jit(solution)/shard_map/ppermute | solution.py:412
  112.0 7.3 %shard_map.123 = (bf16[1024,1536]{1,0:T(8,128)(2,1)}, bf16[1024,128]{1,0:T(8,128)(2,1)}, bf16[4,1024,256]{2,1,0:T(8,128)(2,1)}, bf16[1024,512]{1,0:T(8,128)(2,1)}) custom-call(s32[33]{0:T(128)} %concatenate.11.place, bf16[16,32,2176]{2,1,0:T(8,128)(2,1)} %copy-done.1, bf16[16,32,2176]{2,1,0:T(8,128)(2,1)} %collective-permute-done.26.far_ref, ...), custom_call_target="tpu_custom_call" | custom-call | flops 2000000000 | bytes 10000000 | tf_op jit(solution)/shard_map/pallas_call | solution.py:458
  119.4 4.9 %collective-permute-start = (bf16[128,512]{1,0:T(8,128)(2,1)S(1)}, bf16[128,512]{1,0:T(8,128)(2,1)S(1)}, u32[]{:S(2)}, u32[]{:S(2)}) collective-permute-start(bf16[128,512]{1,0:T(8,128)(2,1)S(1)} %get-tuple-element.29), channel_id=1, source_target_pairs={{0,4},{4,8},{8,12},{12,16},{16,20},{20,24},{24,28},{28,0},{1,5},{5... | collective-permute-start | bytes 393224 | tf_op jit(solution)/shard_map/ppermute | solution.py:412
  124.4 2.9 %collective-permute-done.8.refs_2_ = bf16[192,768]{1,0:T(8,128)(2,1)} collective-permute-done((bf16[192,768]{1,0:T(8,128)(2,1)}, bf16[192,768]{1,0:T(8,128)(2,1)}, u32[]{:S(2)}, u32[]{:S(2)}) %collective-permute-start.8) | collective-permute-done | bytes 294944 | tf_op jit(solution)/shard_map/ppermute | solution.py:412
  128.2 20.2 %collective-permute-done.9.refs_3_ = bf16[192,768]{1,0:T(8,128)(2,1)S(1)} collective-permute-done((bf16[192,768]{1,0:T(8,128)(2,1)}, bf16[192,768]{1,0:T(8,128)(2,1)S(1)}, u32[]{:S(2)}, u32[]{:S(2)}) %collective-permute-start.9) | collective-permute-done | bytes 294944 | tf_op jit(solution)/shard_map/ppermute | solution.py:412
  149.1 9.1 %shard_map.124 = (bf16[1024,768]{1,0:T(8,128)(2,1)}, f32[1024,768]{1,0:T(8,128)}, bf16[1536,768]{1,0:T(8,128)(2,1)}) custom-call(s32[8]{0:T(128)} %stack.146.place, bf16[192,768]{1,0:T(8,128)(2,1)} %get-tuple-element.22.refs_0_, bf16[192,768]{1,0:T(8,128)(2,1)} %collective-permute-done.7.refs_1_, bf16[192,768]{1,0:T(8,128)(2,1)} %collective-permute-done.8.refs_2_, ...), custom_call_target="tpu_custom_call" | custom-call | flops 3000000000 | bytes 10000000 | tf_op jit(solution)/shard_map/pallas_call | solution.py:487
  159.4 11.7 %shard_map.125.refs_8_ = f32[64,4,128,128]{3,2,1,0:T(8,128)} custom-call(s32[8,8]{1,0:T(8,128)} %mask.3, bf16[1024,768]{1,0:T(8,128)(2,1)} %get-tuple-element.10.q_ref, bf16[4,1024,256]{2,1,0:T(8,128)(2,1)} %get-tuple-element.11.wide_ref.refs_11_), custom_call_target="tpu_custom_call" | custom-call | flops 2000000000 | bytes 10000000 | tf_op jit(solution)/shard_map/pallas_call | solution.py:509
  172.0 17.4 %shard_map.126 = f32[8,24,128]{2,1,0:T(8,128)} custom-call(s32[8,8]{1,0:T(8,128)} %mask.3, s32[8]{0:T(128)} %stack.146.place, bf16[128,512]{1,0:T(8,128)(2,1)} %get-tuple-element.30.refs_0_, bf16[128,512]{1,0:T(8,128)(2,1)} %copy-done.3, bf16[128,512]{1,0:T(8,128)(2,1)} %copy-done.4, bf16[128,512]{1,0:T(8,128)(2,1)} %copy-done.5, ...), custom_call_target="tpu_custom_call" | custom-call | flops 4000000000 | bytes 10000000 | tf_op jit(solution)/shard_map/pallas_call | solution.py:528
  189.4 5.3 %all-to-all-start = ((f32[8,24,128]{2,1,0:T(8,128)}), f32[8,24,128]{2,1,0:T(8,128)S(1)}, u32[]{:S(2)}, u32[]{:S(2)}) async-start(f32[8,24,128]{2,1,0:T(8,128)} %shard_map.126), calls=%async_computation | async-start | bytes 196608 | tf_op jit(solution)/shard_map/all_to_all | solution.py:561
  194.8 7.1 %all-to-all-done = f32[8,24,128]{2,1,0:T(8,128)S(1)} async-done(((f32[8,24,128]{2,1,0:T(8,128)}), f32[8,24,128]{2,1,0:T(8,128)S(1)}, u32[]{:S(2)}, u32[]{:S(2)}) %all-to-all-start) | async-done | bytes 98336 | tf_op jit(solution)/shard_map/all_to_all | solution.py:561
  202.0 1.6 collective-permute-start.28
  (105 shorter events, 16.8 us)
Async XLA Ops:
  5.1 9.9 %collective-permute-start.21 = (bf16[32,2176]{1,0:T(8,128)(2,1)}, bf16[32,2176]{1,0:T(8,128)(2,1)S(1)}, u32[]{:S(2)}, u32[]{:S(2)}) collective-permute-start(bf16[32,2176]{1,0:T(8,128)(2,1)} %shard_map.122), channel_id=1, source_target_pairs={{0,8},{4,12},{8,16},{12,20},{16,24},{20,28},{24,0},{28,4},{1,9},{5... | collective-permute-start | bytes 417800 | tf_op jit(solution)/shard_map/ppermute | solution.py:412
  8.2 12.0 %collective-permute-start.22 = (bf16[32,2176]{1,0:T(8,128)(2,1)}, bf16[32,2176]{1,0:T(8,128)(2,1)S(1)}, u32[]{:S(2)}, u32[]{:S(2)}) collective-permute-start(bf16[32,2176]{1,0:T(8,128)(2,1)} %shard_map.122), channel_id=1, source_target_pairs={{0,16},{4,20},{8,24},{12,28},{16,0},{20,4},{24,8},{28,12},{1,17},{... | collective-permute-start | bytes 417800 | tf_op jit(solution)/shard_map/ppermute | solution.py:412
  10.8 9.4 %collective-permute-start.23 = (bf16[32,2176]{1,0:T(8,128)(2,1)}, bf16[32,2176]{1,0:T(8,128)(2,1)S(1)}, u32[]{:S(2)}, u32[]{:S(2)}) collective-permute-start(bf16[32,2176]{1,0:T(8,128)(2,1)} %shard_map.122), channel_id=1, source_target_pairs={{0,24},{4,28},{8,0},{12,4},{16,8},{20,12},{24,16},{28,20},{1,25},{... | collective-permute-start | bytes 417800 | tf_op jit(solution)/shard_map/ppermute | solution.py:412
  21.2 14.5 %collective-permute-start.24 = (bf16[4,32,2176]{2,1,0:T(8,128)(2,1)S(1)}, bf16[4,32,2176]{2,1,0:T(8,128)(2,1)S(1)}, u32[]{:S(2)}, u32[]{:S(2)}) collective-permute-start(bf16[4,32,2176]{2,1,0:T(8,128)(2,1)S(1)} %pad_maximum_fusion), channel_id=1, source_target_pairs={{0,4},{4,0},{8,12},{12,8},{16,20},{20,16},{24,28},{28,24},{1,5},{5... | collective-permute-start | bytes 1671176 | tf_op jit(solution)/shard_map/ppermute | solution.py:412
  35.8 25.6 %collective-permute-start.25 = (bf16[8,32,2176]{2,1,0:T(8,128)(2,1)S(1)}, bf16[8,32,2176]{2,1,0:T(8,128)(2,1)S(1)}, u32[]{:S(2)}, u32[]{:S(2)}) collective-permute-start(bf16[8,32,2176]{2,1,0:T(8,128)(2,1)S(1)} %get-tuple-element.32), channel_id=1, source_target_pairs={{0,2},{1,3},{2,0},{3,1},{4,6},{5,7},{6,4},{7,5},{8,10},{9,11},{10,... | collective-permute-start | bytes 3342344 | tf_op jit(solution)/shard_map/ppermute | solution.py:412
  61.6 47.0 %collective-permute-start.26 = (bf16[16,32,2176]{2,1,0:T(8,128)(2,1)S(1)}, bf16[16,32,2176]{2,1,0:T(8,128)(2,1)}, u32[]{:S(2)}, u32[]{:S(2)}) collective-permute-start(bf16[16,32,2176]{2,1,0:T(8,128)(2,1)S(1)} %constant_dynamic-update-slice_fusion.5.near_ref), channel_id=1, source_target_pairs={{0,1},{1,0},{2,3},{3,2},{4,5},{5,4},{6,7},{7,6},{8,9},{9,8},{10,11... | collective-permute-start | bytes 6684680 | tf_op jit(solution)/shard_map/ppermute | solution.py:412
  61.8 49.5 %copy-start.2 = (bf16[128,4096]{1,0:T(8,128)(2,1)S(1)}, bf16[128,4096]{1,0:T(8,128)(2,1)}, u32[]{:S(2)}) copy-start(bf16[128,4096]{1,0:T(8,128)(2,1)} %param.20) | copy-start | bytes 3145732
  65.5 42.2 %collective-permute-start.10 = (bf16[192,768]{1,0:T(8,128)(2,1)}, bf16[192,768]{1,0:T(8,128)(2,1)}, u32[]{:S(2)}, u32[]{:S(2)}) collective-permute-start(bf16[192,768]{1,0:T(8,128)(2,1)} %get-tuple-element.18), channel_id=1, source_target_pairs={{0,16},{4,20},{8,24},{12,28},{16,0},{20,4},{24,8},{28,12},{1,17},{... | collective-permute-start | bytes 884744 | tf_op jit(solution)/shard_map/ppermute | solution.py:412
  68.3 39.8 %collective-permute-start.11 = (bf16[192,768]{1,0:T(8,128)(2,1)}, bf16[192,768]{1,0:T(8,128)(2,1)}, u32[]{:S(2)}, u32[]{:S(2)}) collective-permute-start(bf16[192,768]{1,0:T(8,128)(2,1)} %get-tuple-element.17), channel_id=1, source_target_pairs={{0,20},{4,24},{8,28},{12,0},{16,4},{20,8},{24,12},{28,16},{1,21},{... | collective-permute-start | bytes 884744 | tf_op jit(solution)/shard_map/ppermute | solution.py:412
  70.0 16.0 %collective-permute-start.14 = (f32[1,768]{1,0:T(1,128)S(1)}, f32[1,768]{1,0:T(1,128)S(1)}, u32[]{:S(2)}, u32[]{:S(2)}) collective-permute-start(f32[1,768]{1,0:T(1,128)S(1)} %get-tuple-element.47), channel_id=1, source_target_pairs={{0,4},{4,8},{8,12},{12,16},{16,20},{20,24},{24,28},{28,0},{1,5},{5... | collective-permute-start | bytes 9224 | tf_op jit(solution)/shard_map/ppermute | solution.py:412
  73.6 16.1 %collective-permute-start.15 = (f32[1,768]{1,0:T(1,128)S(1)}, f32[1,768]{1,0:T(1,128)S(1)}, u32[]{:S(2)}, u32[]{:S(2)}) collective-permute-start(f32[1,768]{1,0:T(1,128)S(1)} %get-tuple-element.46), channel_id=1, source_target_pairs={{0,8},{4,12},{8,16},{12,20},{16,24},{20,28},{24,0},{28,4},{1,9},{5... | collective-permute-start | bytes 9224 | tf_op jit(solution)/shard_map/ppermute | solution.py:412
  85.9 11.0 %collective-permute-start.16 = (f32[1,768]{1,0:T(1,128)S(1)}, f32[1,768]{1,0:T(1,128)S(1)}, u32[]{:S(2)}, u32[]{:S(2)}) collective-permute-start(f32[1,768]{1,0:T(1,128)S(1)} %get-tuple-element.45), channel_id=1, source_target_pairs={{0,12},{4,16},{8,20},{12,24},{16,28},{20,0},{24,4},{28,8},{1,13},{... | collective-permute-start | bytes 9224 | tf_op jit(solution)/shard_map/ppermute | solution.py:412
  89.7 8.8 %collective-permute-start.17 = (f32[1,768]{1,0:T(1,128)S(1)}, f32[1,768]{1,0:T(1,128)S(1)}, u32[]{:S(2)}, u32[]{:S(2)}) collective-permute-start(f32[1,768]{1,0:T(1,128)S(1)} %get-tuple-element.44), channel_id=1, source_target_pairs={{0,16},{4,20},{8,24},{12,28},{16,0},{20,4},{24,8},{28,12},{1,17},{... | collective-permute-start | bytes 9224 | tf_op jit(solution)/shard_map/ppermute | solution.py:412
  96.9 4.5 %collective-permute-start.18 = (f32[1,768]{1,0:T(1,128)S(1)}, f32[1,768]{1,0:T(1,128)S(1)}, u32[]{:S(2)}, u32[]{:S(2)}) collective-permute-start(f32[1,768]{1,0:T(1,128)S(1)} %get-tuple-element.43), channel_id=1, source_target_pairs={{0,20},{4,24},{8,28},{12,0},{16,4},{20,8},{24,12},{28,16},{1,21},{... | collective-permute-start | bytes 9224 | tf_op jit(solution)/shard_map/ppermute | solution.py:412
  98.5 4.2 %collective-permute-start.19 = (f32[1,768]{1,0:T(1,128)S(1)}, f32[1,768]{1,0:T(1,128)S(1)}, u32[]{:S(2)}, u32[]{:S(2)}) collective-permute-start(f32[1,768]{1,0:T(1,128)S(1)} %get-tuple-element.49), channel_id=1, source_target_pairs={{0,24},{4,28},{8,0},{12,4},{16,8},{20,12},{24,16},{28,20},{1,25},{... | collective-permute-start | bytes 9224 | tf_op jit(solution)/shard_map/ppermute | solution.py:412
  101.4 4.6 %collective-permute-start.20 = (f32[1,768]{1,0:T(1,128)S(1)}, f32[1,768]{1,0:T(1,128)S(1)}, u32[]{:S(2)}, u32[]{:S(2)}) collective-permute-start(f32[1,768]{1,0:T(1,128)S(1)} %get-tuple-element.42), channel_id=1, source_target_pairs={{0,28},{4,0},{8,4},{12,8},{16,12},{20,16},{24,20},{28,24},{1,29},{... | collective-permute-start | bytes 9224 | tf_op jit(solution)/shard_map/ppermute | solution.py:412
  102.7 16.6 %collective-permute-start.12 = (bf16[192,768]{1,0:T(8,128)(2,1)}, bf16[192,768]{1,0:T(8,128)(2,1)S(1)}, u32[]{:S(2)}, u32[]{:S(2)}) collective-permute-start(bf16[192,768]{1,0:T(8,128)(2,1)} %get-tuple-element.23), channel_id=1, source_target_pairs={{0,24},{4,28},{8,0},{12,4},{16,8},{20,12},{24,16},{28,20},{1,25},{... | collective-permute-start | bytes 884744 | tf_op jit(solution)/shard_map/ppermute | solution.py:412
  106.0 18.3 %collective-permute-start.13 = (bf16[192,768]{1,0:T(8,128)(2,1)}, bf16[192,768]{1,0:T(8,128)(2,1)S(1)}, u32[]{:S(2)}, u32[]{:S(2)}) collective-permute-start(bf16[192,768]{1,0:T(8,128)(2,1)} %get-tuple-element.16), channel_id=1, source_target_pairs={{0,28},{4,0},{8,4},{12,8},{16,12},{20,16},{24,20},{28,24},{1,29},{... | collective-permute-start | bytes 884744 | tf_op jit(solution)/shard_map/ppermute | solution.py:412
  107.7 16.6 %collective-permute-start.7 = (bf16[192,768]{1,0:T(8,128)(2,1)}, bf16[192,768]{1,0:T(8,128)(2,1)}, u32[]{:S(2)}, u32[]{:S(2)}) collective-permute-start(bf16[192,768]{1,0:T(8,128)(2,1)} %get-tuple-element.21), channel_id=1, source_target_pairs={{0,4},{4,8},{8,12},{12,16},{16,20},{20,24},{24,28},{28,0},{1,5},{5... | collective-permute-start | bytes 884744 | tf_op jit(solution)/shard_map/ppermute | solution.py:412
  108.0 19.2 %collective-permute-start.8 = (bf16[192,768]{1,0:T(8,128)(2,1)}, bf16[192,768]{1,0:T(8,128)(2,1)}, u32[]{:S(2)}, u32[]{:S(2)}) collective-permute-start(bf16[192,768]{1,0:T(8,128)(2,1)} %get-tuple-element.20), channel_id=1, source_target_pairs={{0,8},{4,12},{8,16},{12,20},{16,24},{20,28},{24,0},{28,4},{1,9},{5... | collective-permute-start | bytes 884744 | tf_op jit(solution)/shard_map/ppermute | solution.py:412
  108.6 39.8 %collective-permute-start.9 = (bf16[192,768]{1,0:T(8,128)(2,1)}, bf16[192,768]{1,0:T(8,128)(2,1)S(1)}, u32[]{:S(2)}, u32[]{:S(2)}) collective-permute-start(bf16[192,768]{1,0:T(8,128)(2,1)} %get-tuple-element.19), channel_id=1, source_target_pairs={{0,12},{4,16},{8,20},{12,24},{16,28},{20,0},{24,4},{28,8},{1,13},{... | collective-permute-start | bytes 884744 | tf_op jit(solution)/shard_map/ppermute | solution.py:412
  119.4 38.8 %collective-permute-start = (bf16[128,512]{1,0:T(8,128)(2,1)S(1)}, bf16[128,512]{1,0:T(8,128)(2,1)S(1)}, u32[]{:S(2)}, u32[]{:S(2)}) collective-permute-start(bf16[128,512]{1,0:T(8,128)(2,1)S(1)} %get-tuple-element.29), channel_id=1, source_target_pairs={{0,4},{4,8},{8,12},{12,16},{16,20},{20,24},{24,28},{28,0},{1,5},{5... | collective-permute-start | bytes 393224 | tf_op jit(solution)/shard_map/ppermute | solution.py:412
  124.3 34.0 %collective-permute-start.1 = (bf16[128,512]{1,0:T(8,128)(2,1)S(1)}, bf16[128,512]{1,0:T(8,128)(2,1)S(1)}, u32[]{:S(2)}, u32[]{:S(2)}) collective-permute-start(bf16[128,512]{1,0:T(8,128)(2,1)S(1)} %get-tuple-element.28), channel_id=1, source_target_pairs={{0,8},{4,12},{8,16},{12,20},{16,24},{20,28},{24,0},{28,4},{1,9},{5... | collective-permute-start | bytes 393224 | tf_op jit(solution)/shard_map/ppermute | solution.py:412
  124.3 46.9 %collective-permute-start.2 = (bf16[128,512]{1,0:T(8,128)(2,1)S(1)}, bf16[128,512]{1,0:T(8,128)(2,1)S(1)}, u32[]{:S(2)}, u32[]{:S(2)}) collective-permute-start(bf16[128,512]{1,0:T(8,128)(2,1)S(1)} %get-tuple-element.27), channel_id=1, source_target_pairs={{0,12},{4,16},{8,20},{12,24},{16,28},{20,0},{24,4},{28,8},{1,13},{... | collective-permute-start | bytes 393224 | tf_op jit(solution)/shard_map/ppermute | solution.py:412
  127.3 43.9 %collective-permute-start.3 = (bf16[128,512]{1,0:T(8,128)(2,1)S(1)}, bf16[128,512]{1,0:T(8,128)(2,1)S(1)}, u32[]{:S(2)}, u32[]{:S(2)}) collective-permute-start(bf16[128,512]{1,0:T(8,128)(2,1)S(1)} %get-tuple-element.26), channel_id=1, source_target_pairs={{0,16},{4,20},{8,24},{12,28},{16,0},{20,4},{24,8},{28,12},{1,17},{... | collective-permute-start | bytes 393224 | tf_op jit(solution)/shard_map/ppermute | solution.py:412
  148.4 22.8 %collective-permute-start.4 = (bf16[128,512]{1,0:T(8,128)(2,1)S(1)}, bf16[128,512]{1,0:T(8,128)(2,1)S(1)}, u32[]{:S(2)}, u32[]{:S(2)}) collective-permute-start(bf16[128,512]{1,0:T(8,128)(2,1)S(1)} %get-tuple-element.25), channel_id=1, source_target_pairs={{0,20},{4,24},{8,28},{12,0},{16,4},{20,8},{24,12},{28,16},{1,21},{... | collective-permute-start | bytes 393224 | tf_op jit(solution)/shard_map/ppermute | solution.py:412
  158.2 13.0 %collective-permute-start.5 = (bf16[128,512]{1,0:T(8,128)(2,1)S(1)}, bf16[128,512]{1,0:T(8,128)(2,1)S(1)}, u32[]{:S(2)}, u32[]{:S(2)}) collective-permute-start(bf16[128,512]{1,0:T(8,128)(2,1)S(1)} %get-tuple-element.31), channel_id=1, source_target_pairs={{0,24},{4,28},{8,0},{12,4},{16,8},{20,12},{24,16},{28,20},{1,25},{... | collective-permute-start | bytes 393224 | tf_op jit(solution)/shard_map/ppermute | solution.py:412
  158.3 12.9 %collective-permute-start.6 = (bf16[128,512]{1,0:T(8,128)(2,1)S(1)}, bf16[128,512]{1,0:T(8,128)(2,1)S(1)}, u32[]{:S(2)}, u32[]{:S(2)}) collective-permute-start(bf16[128,512]{1,0:T(8,128)(2,1)S(1)} %get-tuple-element.24), channel_id=1, source_target_pairs={{0,28},{4,0},{8,4},{12,8},{16,12},{20,16},{24,20},{28,24},{1,29},{... | collective-permute-start | bytes 393224 | tf_op jit(solution)/shard_map/ppermute | solution.py:412
  189.4 12.5 %all-to-all-start = ((f32[8,24,128]{2,1,0:T(8,128)}), f32[8,24,128]{2,1,0:T(8,128)S(1)}, u32[]{:S(2)}, u32[]{:S(2)}) async-start(f32[8,24,128]{2,1,0:T(8,128)} %shard_map.126), calls=%async_computation | async-start | bytes 196608 | tf_op jit(solution)/shard_map/all_to_all | solution.py:561
  201.9 2.8 %collective-permute-start.27 = (f32[13,128]{1,0:T(8,128)S(1)}, f32[13,128]{1,0:T(8,128)S(1)}, u32[]{:S(2)}, u32[]{:S(2)}) collective-permute-start(f32[13,128]{1,0:T(8,128)S(1)} %slice_reduce_fusion), channel_id=1, source_target_pairs={{0,1},{1,0},{2,3},{3,2},{4,5},{5,4},{6,7},{7,6},{8,9},{9,8},{10,11... | collective-permute-start | bytes 19976 | tf_op jit(solution)/shard_map/ppermute | solution.py:567
  202.0 3.7 %collective-permute-start.28 = (f32[13,128]{1,0:T(8,128)S(1)}, f32[13,128]{1,0:T(8,128)S(1)}, u32[]{:S(2)}, u32[]{:S(2)}) collective-permute-start(f32[13,128]{1,0:T(8,128)S(1)} %slice_reduce_fusion), channel_id=1, source_target_pairs={{0,2},{1,3},{2,0},{3,1},{4,6},{5,7},{6,4},{7,5},{8,10},{9,11},{10,... | collective-permute-start | bytes 19976 | tf_op jit(solution)/shard_map/ppermute | solution.py:567
  203.5 3.1 %collective-permute-start.29 = (f32[13,128]{1,0:T(8,128)S(1)}, f32[13,128]{1,0:T(8,128)S(1)}, u32[]{:S(2)}, u32[]{:S(2)}) collective-permute-start(f32[13,128]{1,0:T(8,128)S(1)} %slice_reduce_fusion), channel_id=1, source_target_pairs={{0,3},{1,2},{2,1},{3,0},{4,7},{5,6},{6,5},{7,4},{8,11},{9,10},{10,... | collective-permute-start | bytes 19976 | tf_op jit(solution)/shard_map/ppermute | solution.py:567
  (22 other events, 338.1 us)
